TPU v7x, 32 devices: a whole 2x2x4 slice. The times are simulated.
32 devices in a mesh: grp: 1, lat: 32 (over z, y, x, core).
Axes of the slice: x: 2, y: 2, z: 4, core: 2. Of those that a mesh axis runs over, the one named last changes fastest.
Arguments:
- fields: bfloat16 [768, 64, 2048], P(('grp', 'lat')), may hold values from -6 to 6
- spectral_weight: bfloat16 [2, 128, 64, 128], replicated, may hold values from -0.5 to 0.5
- local_weight: bfloat16 [2, 64, 64], replicated, may hold values from -0.75 to 0.75
Outputs:
- updated: bfloat16 [768, 64, 2048], P(('grp', 'lat'))
All inputs are finite; a program needn't handle non-finite values.
Results may differ from a plain program's by a relative error of at most 0.011.
Values may be sent and summed in bfloat16 or wider, within the bound.
A program may use at most 128 MiB of HBM per device.

v0:
```python
import math

import jax
import jax.numpy as jnp
from jax import lax
from jax.sharding import PartitionSpec as P

KY = 128


def lon_forward_table(lon_count, mode_count):
    cells = jnp.arange(lon_count, dtype=jnp.int32)[:, None]
    modes = jnp.arange(mode_count, dtype=jnp.int32)[None, :]
    angle = 2.0 * jnp.pi / lon_count * (cells * modes % lon_count).astype(jnp.float32)
    factor = 1.0 / math.sqrt(lon_count)
    return jnp.stack([jnp.cos(angle) * factor, -jnp.sin(angle) * factor], axis=1).astype(
        jnp.bfloat16
    )


def lon_back_table(lon_count, mode_count):
    modes = jnp.arange(mode_count, dtype=jnp.int32)[:, None]
    cells = jnp.arange(lon_count, dtype=jnp.int32)[None, :]
    angle = 2.0 * jnp.pi / lon_count * (cells * modes % lon_count).astype(jnp.float32)
    factor = 1.0 / math.sqrt(mode_count)
    return jnp.stack([jnp.cos(angle) * factor, -jnp.sin(angle) * factor], axis=1).astype(
        jnp.bfloat16
    )


def lat_tables(lat_count, kept_count, block_rows):
    index = jnp.arange(kept_count, dtype=jnp.int32)
    waves = jnp.where(index < kept_count // 2, index, lat_count - kept_count + index)
    rowids = jnp.arange(lat_count, dtype=jnp.int32)
    stride = lat_count // block_rows
    latitudes = rowids % block_rows * stride + rowids // block_rows
    angle = (
        2.0
        * jnp.pi
        / lat_count
        * (waves[:, None] * latitudes[None, :] % lat_count).astype(jnp.float32)
    )
    forward = jnp.stack([jnp.cos(angle), jnp.sin(angle)], axis=0) * (1.0 / math.sqrt(lat_count))
    backward = jnp.stack([jnp.cos(angle).T, jnp.sin(angle).T], axis=0) * (
        1.0 / math.sqrt(kept_count)
    )
    return (forward.astype(jnp.bfloat16), backward.astype(jnp.bfloat16))


def lat_forward(table, values, channels):
    products = jnp.einsum("pjn,nkc->pjkc", table, values, preferred_element_type=jnp.float32)
    real_part = products[0, ..., :channels] + products[1, ..., channels:]
    imag_part = products[0, ..., channels:] - products[1, ..., :channels]
    return jnp.concatenate([real_part, imag_part], axis=-1)


def lat_backward(table, modes, channels):
    products = jnp.einsum("pnj,jkc->pnkc", table, modes, preferred_element_type=jnp.float32)
    real_part = products[0, ..., :channels] - products[1, ..., channels:]
    imag_part = products[1, ..., :channels] + products[0, ..., channels:]
    return jnp.concatenate([real_part, imag_part], axis=-1)


def mix_matrix(weight, channels):
    real_w = weight[..., :channels]
    imag_w = weight[..., channels:]
    lower = jnp.concatenate([-imag_w, real_w], axis=-1)
    return jnp.concatenate([weight, lower], axis=1)


def spectral_block(gathered, mixing, forward_lat, backward_lat, channels):
    lat_modes = lat_forward(forward_lat, gathered, channels).astype(jnp.bfloat16)
    mixed_modes = jnp.einsum(
        "jkc,kcd->jkd", lat_modes, mixing, preferred_element_type=jnp.float32
    ).astype(jnp.bfloat16)
    return lat_backward(backward_lat, mixed_modes, channels).astype(jnp.bfloat16)


def shards(fields, spectral_weight, local_weight):
    row_count, channels, lon_count = fields.shape
    layer_count = spectral_weight.shape[0]
    mode_rows = spectral_weight.shape[1]
    devices = lax.axis_size("lat")
    my_index = lax.axis_index("lat")
    lat_count = row_count * devices
    forward_lon = lon_forward_table(lon_count, mode_rows)
    backward_lon = lon_back_table(lon_count, mode_rows)
    forward_lat, backward_lat = lat_tables(lat_count, KY, row_count)
    current = fields
    for layer_idx in range(layer_count):
        mixing = mix_matrix(spectral_weight[layer_idx], channels)
        lon_modes = jnp.einsum(
            "rcl,lpk->rkpc", current, forward_lon, preferred_element_type=jnp.float32
        )
        lon_modes = lon_modes.reshape(row_count, mode_rows, 2 * channels).astype(jnp.bfloat16)
        slice_size = mode_rows // devices
        gathered = lax.all_to_all(lon_modes, "lat", split_axis=1, concat_axis=0, tiled=True)
        my_mixing = lax.dynamic_slice_in_dim(mixing, my_index * slice_size, slice_size, 0)
        rebuilt = spectral_block(gathered, my_mixing, forward_lat, backward_lat, channels)
        lat_back = lax.all_to_all(rebuilt, "lat", split_axis=0, concat_axis=1, tiled=True)
        spectral = jnp.einsum(
            "rkpc,kpl->rcl",
            lat_back.reshape(row_count, mode_rows, 2, channels),
            backward_lon,
            preferred_element_type=jnp.float32,
        )
        pointwise = jnp.einsum(
            "rcl,cd->rdl", current, local_weight[layer_idx], preferred_element_type=jnp.float32
        )
        current = jax.nn.gelu(spectral + pointwise, approximate=True).astype(jnp.bfloat16)
    return current


def solution(mesh):
    return jax.shard_map(
        shards,
        mesh=mesh,
        in_specs=(P(("grp", "lat"), None, None), P(), P()),
        out_specs=P(("grp", "lat"), None, None),
        check_vma=False,
    )
```

profile of v0, /device:TPU:0, one launch (start us, length us, event | category | flops | bytes accessed | tf_op | source)
XLA Modules:
  0.0 144.1 jit_solution(10989742851166684646)
XLA Ops:
  0.0 4.4 %multiply_convert_fusion.2 = (bf16[2048,1,128]{2,0,1:T(8,128)(2,1)S(1)}, bf16[2048,1,128]{2,0,1:T(8,128)(2,1)S(1)}) fusion(), kind=kLoop, calls=%fused_computation.60 | loop fusion | flops 4980736 | bytes 1048576 | tf_op jit(solution)/shard_map/convert.19
  4.5 5.0 %fusion.31 = bf16[24,128,2,64]{1,3,0,2:T(8,128)(2,1)S(1)} fusion(bf16[24,64,2048]{2,1,0:T(8,128)(2,1)} %param.3, bf16[2048,1,128]{2,0,1:T(8,128)(2,1)S(1)} %get-tuple-element.23, bf16[2048,1,128]{2,0,1:T(8,128)(2,1)S(1)} %get-tuple-element.24), kind=kOutput, calls=%fused_computation.43 | convolution fusion | flops 1613103104 | bytes 8126464 | tf_op jit(solution)/shard_map/rcl,lpk->rkpc/dot_general | solution.py:92
  9.4 0.1 copy.26
  9.5 1.3 copy.27
  10.8 7.3 %all-to-all-start = ((bf16[24,128,128]{2,0,1:T(8,128)(2,1)}), bf16[24,128,128]{2,0,1:T(8,128)(2,1)S(1)}, u32[]{:S(2)}, u32[]{:S(2)}) async-start(bf16[24,128,128]{2,0,1:T(8,128)(2,1)} %copy.27), calls=%async_computation | async-start | bytes 1572864 | tf_op jit(solution)/shard_map/all_to_all | solution.py:97
  18.1 4.5 %fusion.150 = (bf16[1,128,64,128]{3,2,1,0:T(8,128)(2,1)}, bf16[1,128,64,128]{3,2,1,0:T(8,128)(2,1)S(1)}) fusion(bf16[2,128,64,128]{3,2,1,0:T(8,128)(2,1)} %param.4), kind=kLoop, calls=%fused_computation.167 | loop fusion | bytes 8388608 | tf_op jit(solution)/shard_map/slice | solution.py:91
  22.6 3.1 %copy.58 = bf16[1,128,64,128]{2,3,1,0:T(8,128)(2,1)} copy(bf16[1,128,64,128]{3,2,1,0:T(8,128)(2,1)S(1)} %get-tuple-element.8) | data formatting | bytes 4194304
  25.7 1.6 %fusion.69 = (f32[1,128,768]{2,1,0:T(8,128)S(1)}, f32[1,128,768]{2,1,0:T(8,128)S(1)}) fusion(s32[768]{0:T(1024)S(1)} %fusion.126, s32[128]{0:T(128)S(1)} %compare_select_fusion), kind=kLoop, calls=%fused_computation.98 | loop fusion | flops 884736 | bytes 790016 | tf_op jit(solution)/shard_map/cos | solution.py:44
  27.4 2.8 %fusion.73 = (f32[1,768,128]{2,1,0:T(8,128)S(1)}, f32[1,768,128]{2,1,0:T(8,128)}) fusion(s32[768]{0:T(1024)S(1)} %fusion.126, s32[128]{0:T(128)S(1)} %compare_select_fusion), kind=kLoop, calls=%fused_computation.103 | loop fusion | flops 884736 | bytes 790016 | tf_op jit(solution)/shard_map/cos | solution.py:44
  30.2 4.6 %fusion.151 = (bf16[128,64,64]{1,2,0:T(8,128)(2,1)}, bf16[128,64,64]{1,2,0:T(8,128)(2,1)}) fusion(bf16[128,64,128]{1,2,0:T(8,128)(2,1)} %bitcast.126), kind=kLoop, calls=%fused_computation.168 | loop fusion | flops 524288 | bytes 4194304 | tf_op jit(solution)/shard_map/slice | solution.py:65
  34.8 3.9 %all-to-all-done = bf16[24,128,128]{2,0,1:T(8,128)(2,1)S(1)} async-done(((bf16[24,128,128]{2,0,1:T(8,128)(2,1)}), bf16[24,128,128]{2,0,1:T(8,128)(2,1)S(1)}, u32[]{:S(2)}, u32[]{:S(2)}) %all-to-all-start) | async-done | bytes 786464 | tf_op jit(solution)/shard_map/all_to_all | solution.py:97
  38.7 0.1 copy.28
  38.8 0.5 fusion.112
  39.3 0.7 fusion.104
  40.0 1.8 %fusion.55 = f32[2,768,4,128]{1,3,2,0:T(8,128)S(1)} fusion(s32[]{:T(128)S(6)} %select_n.128, bf16[128,64,128]{1,2,0:T(8,128)(2,1)} %bitcast.127, bf16[128,64,64]{1,2,0:T(8,128)(2,1)} %get-tuple-element.10, bf16[128,64,64]{1,2,0:T(8,128)(2,1)} %get-tuple-element.9, bf16[128,4,64]{0,2,1:T(8,128)(2,1)} %get-tuple-element.18, ...), kind=kOutput, calls=%fused_computation.83 | convolution fusion | flops 219414528 | bytes 8257540 | tf_op jit(solution)/shard_map/pnj,jkc->pnkc/dot_general | solution.py:58
  41.8 0.2 fusion.62
  42.0 0.1 pad_maximum_fusion
  42.0 1.3 copy.31
  43.3 3.8 %all-to-all-start.1 = ((bf16[768,4,128]{2,1,0:T(4,128)(2,1)}), bf16[768,4,128]{2,1,0:T(4,128)(2,1)S(1)}, u32[]{:S(2)}, u32[]{:S(2)}) async-start(bf16[768,4,128]{2,1,0:T(4,128)(2,1)} %copy.31), calls=%async_computation.1 | async-start | bytes 1572864 | tf_op jit(solution)/shard_map/all_to_all | solution.py:100
  47.1 5.4 %multiply_convert_fusion = (bf16[128,1,2048]{2,0,1:T(8,128)(2,1)}, bf16[128,1,2048]{2,0,1:T(8,128)(2,1)}) fusion(), kind=kLoop, calls=%fused_computation.56 | loop fusion | flops 4980736 | bytes 1048576 | tf_op jit(solution)/shard_map/convert.9
  52.5 9.1 %fusion.116 = f32[64,24,2048]{2,0,1:T(8,128)} fusion(bf16[24,64,2048]{2,1,0:T(8,128)(2,1)} %param.3, bf16[2,64,64]{2,1,0:T(8,128)(2,1)S(1)} %copy-done.12), kind=kOutput, calls=%fused_computation.132 | convolution fusion | flops 402653184 | bytes 18890752 | tf_op jit(solution)/shard_map/rcl,cd->rdl/dot_general | solution.py:107
  61.6 5.9 %all-to-all-done.1 = bf16[768,4,128]{2,1,0:T(4,128)(2,1)S(1)} async-done(((bf16[768,4,128]{2,1,0:T(4,128)(2,1)}), bf16[768,4,128]{2,1,0:T(4,128)(2,1)S(1)}, u32[]{:S(2)}, u32[]{:S(2)}) %all-to-all-start.1) | async-done | bytes 786464 | tf_op jit(solution)/shard_map/all_to_all | solution.py:100
  67.5 0.1 copy.32
  67.6 0.1 copy.33
  67.7 0.7 reshape.429
  68.4 8.1 %fusion.7 = bf16[24,64,2048]{2,1,0:T(8,128)(2,1)S(1)} fusion(f32[64,24,2048]{2,0,1:T(8,128)} %fusion.116, bf16[24,128,2,64]{3,2,0,1:T(2,128)(2,1)S(1)} %reshape.429, bf16[128,1,2048]{2,0,1:T(8,128)(2,1)} %get-tuple-element.25, bf16[128,1,2048]{2,0,1:T(8,128)(2,1)} %get-tuple-element.26), kind=kOutput, calls=%fused_computation.9 | convolution fusion | flops 1642594304 | bytes 20709376 | tf_op jit(solution)/shard_map/rkpc,kpl->rcl/dot_general | solution.py:101
  76.6 1.8 %fusion.28 = bf16[24,128,2,64]{1,3,0,2:T(8,128)(2,1)S(1)} fusion(bf16[24,64,2048]{2,1,0:T(8,128)(2,1)S(1)} %fusion.7, bf16[2048,1,128]{2,0,1:T(8,128)(2,1)S(1)} %copy-done.7, bf16[2048,1,128]{2,0,1:T(8,128)(2,1)S(1)} %copy-done.9), kind=kOutput, calls=%fused_computation.42 | convolution fusion | flops 1613103104 | bytes 8126464 | tf_op jit(solution)/shard_map/rcl,lpk->rkpc/dot_general | solution.py:92
  78.4 0.9 copy-done.1
  79.3 0.1 copy.36
  79.3 1.3 copy.37
  80.7 3.6 %all-to-all-start.2 = ((bf16[24,128,128]{2,0,1:T(8,128)(2,1)}), bf16[24,128,128]{2,0,1:T(8,128)(2,1)S(1)}, u32[]{:S(2)}, u32[]{:S(2)}) async-start(bf16[24,128,128]{2,0,1:T(8,128)(2,1)} %copy.37), calls=%async_computation.2 | async-start | bytes 1572864 | tf_op jit(solution)/shard_map/all_to_all | solution.py:97
  84.3 3.1 %copy.57 = bf16[1,128,64,128]{2,3,1,0:T(8,128)(2,1)} copy(bf16[1,128,64,128]{3,2,1,0:T(8,128)(2,1)S(1)} %copy-done) | data formatting | bytes 4194304
  87.5 4.7 %fusion.149 = (bf16[128,64,64]{1,2,0:T(8,128)(2,1)}, bf16[128,64,64]{1,2,0:T(8,128)(2,1)}) fusion(bf16[128,64,128]{1,2,0:T(8,128)(2,1)} %bitcast.128), kind=kLoop, calls=%fused_computation.166 | loop fusion | flops 524288 | bytes 4194304 | tf_op jit(solution)/shard_map/slice | solution.py:65
  92.2 12.7 %all-to-all-done.2 = bf16[24,128,128]{2,0,1:T(8,128)(2,1)S(1)} async-done(((bf16[24,128,128]{2,0,1:T(8,128)(2,1)}), bf16[24,128,128]{2,0,1:T(8,128)(2,1)S(1)}, u32[]{:S(2)}, u32[]{:S(2)}) %all-to-all-start.2) | async-done | bytes 786464 | tf_op jit(solution)/shard_map/all_to_all | solution.py:97
  104.9 0.1 copy.38
  105.0 0.4 fusion.110
  105.5 0.7 fusion.106
  106.1 1.8 %fusion.54 = f32[2,768,4,128]{1,3,2,0:T(8,128)S(1)} fusion(s32[]{:T(128)S(6)} %select_n.128, bf16[128,64,128]{1,2,0:T(8,128)(2,1)} %bitcast.129, bf16[128,64,64]{1,2,0:T(8,128)(2,1)} %get-tuple-element.6, bf16[128,64,64]{1,2,0:T(8,128)(2,1)} %get-tuple-element.5, bf16[128,4,64]{0,2,1:T(8,128)(2,1)} %get-tuple-element.16, ...), kind=kOutput, calls=%fused_computation.82 | convolution fusion | flops 219414528 | bytes 8257540 | tf_op jit(solution)/shard_map/pnj,jkc->pnkc/dot_general | solution.py:58
  108.0 0.2 fusion.64
  108.1 0.1 pad_maximum_fusion.1
  108.2 1.3 copy.41
  109.5 3.8 %all-to-all-start.3 = ((bf16[768,4,128]{2,1,0:T(4,128)(2,1)}), bf16[768,4,128]{2,1,0:T(4,128)(2,1)S(1)}, u32[]{:S(2)}, u32[]{:S(2)}) async-start(bf16[768,4,128]{2,1,0:T(4,128)(2,1)} %copy.41), calls=%async_computation.3 | async-start | bytes 1572864 | tf_op jit(solution)/shard_map/all_to_all | solution.py:100
  113.3 9.1 %fusion.114 = f32[24,2048,64]{1,2,0:T(8,128)} fusion(bf16[24,64,2048]{2,1,0:T(8,128)(2,1)} %copy-done.1, bf16[2,64,64]{2,1,0:T(8,128)(2,1)S(1)} %copy-done.13), kind=kOutput, calls=%fused_computation.130 | convolution fusion | flops 402653184 | bytes 18890752 | tf_op jit(solution)/shard_map/rcl,cd->rdl/dot_general | solution.py:107
  122.5 11.2 %all-to-all-done.3 = bf16[768,4,128]{2,1,0:T(4,128)(2,1)S(1)} async-done(((bf16[768,4,128]{2,1,0:T(4,128)(2,1)}), bf16[768,4,128]{2,1,0:T(4,128)(2,1)S(1)}, u32[]{:S(2)}, u32[]{:S(2)}) %all-to-all-start.3) | async-done | bytes 786464 | tf_op jit(solution)/shard_map/all_to_all | solution.py:100
  133.7 0.1 copy.42
  133.8 0.1 copy.43
  133.9 0.7 reshape.430
  134.6 9.5 %fusion.15 = bf16[24,64,2048]{2,1,0:T(8,128)(2,1)} fusion(f32[24,2048,64]{1,2,0:T(8,128)} %fusion.114, bf16[24,128,2,64]{3,2,0,1:T(2,128)(2,1)S(1)} %reshape.430, bf16[128,1,2048]{2,0,1:T(8,128)(2,1)S(1)} %copy-done.10, bf16[128,1,2048]{2,0,1:T(8,128)(2,1)S(1)} %copy-done.11), kind=kOutput, calls=%fused_computation.17 | convolution fusion | flops 1642594304 | bytes 20709376 | tf_op jit(solution)/shard_map/rkpc,kpl->rcl/dot_general | solution.py:101
  (29 shorter events, 0.1 us)
Async XLA Ops:
  4.4 5.0 %copy-start.6 = (bf16[2048,1,128]{2,0,1:T(8,128)(2,1)}, bf16[2048,1,128]{2,0,1:T(8,128)(2,1)S(1)}, u32[]{:S(2)}) copy-start(bf16[2048,1,128]{2,0,1:T(8,128)(2,1)S(1)} %get-tuple-element.23) | copy-start | bytes 1572868
  4.4 5.0 %copy-start.8 = (bf16[2048,1,128]{2,0,1:T(8,128)(2,1)}, bf16[2048,1,128]{2,0,1:T(8,128)(2,1)S(1)}, u32[]{:S(2)}) copy-start(bf16[2048,1,128]{2,0,1:T(8,128)(2,1)S(1)} %get-tuple-element.24) | copy-start | bytes 1572868
  10.8 27.9 %all-to-all-start = ((bf16[24,128,128]{2,0,1:T(8,128)(2,1)}), bf16[24,128,128]{2,0,1:T(8,128)(2,1)S(1)}, u32[]{:S(2)}, u32[]{:S(2)}) async-start(bf16[24,128,128]{2,0,1:T(8,128)(2,1)} %copy.27), calls=%async_computation | async-start | bytes 1572864 | tf_op jit(solution)/shard_map/all_to_all | solution.py:97
  27.4 11.4 %copy-start.2 = (f32[1,128,768]{2,1,0:T(8,128)}, f32[1,128,768]{2,1,0:T(8,128)S(1)}, u32[]{:S(2)}) copy-start(f32[1,128,768]{2,1,0:T(8,128)S(1)} %get-tuple-element.21) | copy-start | bytes 1179652
  27.4 11.4 %copy-start.4 = (f32[1,128,768]{2,1,0:T(8,128)}, f32[1,128,768]{2,1,0:T(8,128)S(1)}, u32[]{:S(2)}) copy-start(f32[1,128,768]{2,1,0:T(8,128)S(1)} %get-tuple-element.22) | copy-start | bytes 1179652
  41.9 10.5 %copy-start.12 = (bf16[2,64,64]{2,1,0:T(8,128)(2,1)S(1)}, bf16[2,64,64]{2,1,0:T(8,128)(2,1)}, u32[]{:S(2)}) copy-start(bf16[2,64,64]{2,1,0:T(8,128)(2,1)} %param.5) | copy-start | bytes 49156
  43.3 24.2 %all-to-all-start.1 = ((bf16[768,4,128]{2,1,0:T(4,128)(2,1)}), bf16[768,4,128]{2,1,0:T(4,128)(2,1)S(1)}, u32[]{:S(2)}, u32[]{:S(2)}) async-start(bf16[768,4,128]{2,1,0:T(4,128)(2,1)} %copy.31), calls=%async_computation.1 | async-start | bytes 1572864 | tf_op jit(solution)/shard_map/all_to_all | solution.py:100
  68.4 8.1 %copy-start.7 = (bf16[2048,1,128]{2,0,1:T(8,128)(2,1)S(1)}, bf16[2048,1,128]{2,0,1:T(8,128)(2,1)}, u32[]{:S(2)}) copy-start(bf16[2048,1,128]{2,0,1:T(8,128)(2,1)} %copy-done.6) | copy-start | bytes 1572868
  68.4 8.1 %copy-start.9 = (bf16[2048,1,128]{2,0,1:T(8,128)(2,1)S(1)}, bf16[2048,1,128]{2,0,1:T(8,128)(2,1)}, u32[]{:S(2)}) copy-start(bf16[2048,1,128]{2,0,1:T(8,128)(2,1)} %copy-done.8) | copy-start | bytes 1572868
  76.6 2.7 %copy-start.1 = (bf16[24,64,2048]{2,1,0:T(8,128)(2,1)}, bf16[24,64,2048]{2,1,0:T(8,128)(2,1)S(1)}, u32[]{:S(2)}) copy-start(bf16[24,64,2048]{2,1,0:T(8,128)(2,1)S(1)} %fusion.7) | copy-start | bytes 18874372
  79.3 5.0 %copy-start = (bf16[1,128,64,128]{3,2,1,0:T(8,128)(2,1)S(1)}, bf16[1,128,64,128]{3,2,1,0:T(8,128)(2,1)}, u32[]{:S(2)}) copy-start(bf16[1,128,64,128]{3,2,1,0:T(8,128)(2,1)} %get-tuple-element.7) | copy-start | bytes 6291460
  80.7 24.2 %all-to-all-start.2 = ((bf16[24,128,128]{2,0,1:T(8,128)(2,1)}), bf16[24,128,128]{2,0,1:T(8,128)(2,1)S(1)}, u32[]{:S(2)}, u32[]{:S(2)}) async-start(bf16[24,128,128]{2,0,1:T(8,128)(2,1)} %copy.37), calls=%async_computation.2 | async-start | bytes 1572864 | tf_op jit(solution)/shard_map/all_to_all | solution.py:97
  87.5 17.5 %copy-start.3 = (f32[1,128,768]{2,1,0:T(8,128)S(1)}, f32[1,128,768]{2,1,0:T(8,128)}, u32[]{:S(2)}) copy-start(f32[1,128,768]{2,1,0:T(8,128)} %copy-done.2) | copy-start | bytes 1179652
  87.5 17.5 %copy-start.5 = (f32[1,128,768]{2,1,0:T(8,128)S(1)}, f32[1,128,768]{2,1,0:T(8,128)}, u32[]{:S(2)}) copy-start(f32[1,128,768]{2,1,0:T(8,128)} %copy-done.4) | copy-start | bytes 1179652
  108.0 5.4 %copy-start.13 = (bf16[2,64,64]{2,1,0:T(8,128)(2,1)S(1)}, bf16[2,64,64]{2,1,0:T(8,128)(2,1)}, u32[]{:S(2)}) copy-start(bf16[2,64,64]{2,1,0:T(8,128)(2,1)} %param.5) | copy-start | bytes 49156
  109.5 24.2 %all-to-all-start.3 = ((bf16[768,4,128]{2,1,0:T(4,128)(2,1)}), bf16[768,4,128]{2,1,0:T(4,128)(2,1)S(1)}, u32[]{:S(2)}, u32[]{:S(2)}) async-start(bf16[768,4,128]{2,1,0:T(4,128)(2,1)} %copy.41), calls=%async_computation.3 | async-start | bytes 1572864 | tf_op jit(solution)/shard_map/all_to_all | solution.py:100
  122.5 12.2 %copy-start.10 = (bf16[128,1,2048]{2,0,1:T(8,128)(2,1)S(1)}, bf16[128,1,2048]{2,0,1:T(8,128)(2,1)}, u32[]{:S(2)}) copy-start(bf16[128,1,2048]{2,0,1:T(8,128)(2,1)} %get-tuple-element.25) | copy-start | bytes 1572868
  122.5 12.2 %copy-start.11 = (bf16[128,1,2048]{2,0,1:T(8,128)(2,1)S(1)}, bf16[128,1,2048]{2,0,1:T(8,128)(2,1)}, u32[]{:S(2)}) copy-start(bf16[128,1,2048]{2,0,1:T(8,128)(2,1)} %get-tuple-element.26) | copy-start | bytes 1572868
where the time goes:
time: 145 us; the launch traced here: 144 us
  matrix products  47.2 us (33%)
  waiting for transfers between devices  33.8 us (23%)
  other arithmetic  25.3 us (17%)
  local copies, waits for them, and re-layouts  18.9 us (13%)
  starting transfers between devices  18.6 us (13%)
    dot_general x2, matrix products, shards(): jnp.einsum('rcl,cd->rdl', current, local_weight[layer_idx], preferred_ele...  18.2 us
    dot_general x2, matrix products, shards(): jnp.einsum('rkpc,kpl->rcl', lat_back.reshape(row_count, mode_rows, 2, cha...  17.6 us
    all_to_all x2, waiting for transfers between devices, shards(): lax.all_to_all(rebuilt, 'lat', split_axis=0, concat_axis=1, tiled=True)  17.2 us
    all_to_all x2, waiting for transfers between devices, shards(): lax.all_to_all(lon_modes, 'lat', split_axis=1, concat_axis=0, tiled=True)  16.6 us
    all_to_all x2, starting transfers between devices, shards(): lax.all_to_all(lon_modes, 'lat', split_axis=1, concat_axis=0, tiled=True)  11 us
    another operation x2, other arithmetic  9.78 us
    slice x2, other arithmetic, mix_matrix(): real_w = weight[..., :channels]  9.35 us
    all_to_all x2, starting transfers between devices, shards(): lax.all_to_all(rebuilt, 'lat', split_axis=0, concat_axis=1, tiled=True)  7.64 us
  transfers between devices with their start and end apart: 4, of which 4 were waited for; matrix products, arithmetic and copies ran while one was open for 33% of the time, Pallas kernels for 0%

commit v1 on v0

v1 whole, which is shorter than its diff:
```python
import functools
import math

import jax
import jax.numpy as jnp
import numpy as np
from jax import lax
from jax.experimental import pallas as pl
from jax.experimental.pallas import tpu as pltpu
from jax.sharding import PartitionSpec as P

KY = 128
MESH = pl.DeviceIdType.MESH


def lon_table(lon_count, mode_count):
    cells = np.arange(lon_count, dtype=np.int64)[:, None]
    modes = np.arange(mode_count, dtype=np.int64)[None, :]
    angle = (2.0 * np.pi / lon_count) * (cells * modes % lon_count)
    return np.stack([np.cos(angle), -np.sin(angle)], axis=1)


def lat_tables(devices, group, row_count, kept):
    lat_count = devices * row_count
    outer = devices // group
    index = np.arange(kept, dtype=np.int64)
    waves = np.where(index < kept // 2, index, lat_count - kept + index)
    device = np.arange(outer)[:, None, None] * group + np.arange(group)[None, :, None]
    latitudes = (np.arange(row_count)[None, None, :] * devices + device).reshape(outer, -1)
    angle = (2.0 * np.pi / lat_count) * (waves[None, :, None] * latitudes[:, None, :] % lat_count)
    both = np.concatenate([np.cos(angle), np.sin(angle)], axis=1) / math.sqrt(lat_count)
    turned = angle.transpose(0, 2, 1)
    back = np.concatenate([np.cos(turned), np.sin(turned)], axis=1) / math.sqrt(kept)
    return both, back


def lat_kernel(
    group, outer, steps, rows, kept, channels,
    x_ref, mix_ref, fwd_ref, bwd_ref, y_ref,
    r_buf, p_buf, q_buf, m_buf, v_buf,
    local_sem, a_send, a_recv, b_send, b_recv, c_send, c_recv, d_send, d_recv,
):
    me = lax.axis_index("lat")
    z = me // group
    s = lax.rem(me, group)
    rows_all = rows * group

    def inner_peer(i):
        return lax.rem(s + i, group)

    def outer_peer(i):
        return lax.rem(z + i, outer)

    barrier = pltpu.get_barrier_semaphore()
    for i in range(1, group):
        pl.semaphore_signal(
            barrier, inc=1, device_id={"lat": z * group + inner_peer(i)}, device_id_type=MESH
        )
    for i in range(1, outer):
        pl.semaphore_signal(
            barrier, inc=1, device_id={"lat": outer_peer(i) * group + s}, device_id_type=MESH
        )

    def block(who):
        return pl.ds(pl.multiple_of(who * rows, 8), rows)

    def a_copy(t, i):
        to = inner_peer(i)
        return pltpu.make_async_remote_copy(
            src_ref=x_ref.at[pl.ds((to * steps + t) * outer, outer)],
            dst_ref=r_buf.at[t, :, block(s)],
            send_sem=a_send.at[t, i], recv_sem=a_recv.at[t, i],
            device_id={"lat": z * group + to}, device_id_type=MESH,
        )

    def b_copy(t, i):
        to = outer_peer(i)
        return pltpu.make_async_remote_copy(
            src_ref=p_buf.at[t, to], dst_ref=q_buf.at[t, z],
            send_sem=b_send.at[t, i], recv_sem=b_recv.at[t, i],
            device_id={"lat": to * group + s}, device_id_type=MESH,
        )

    def c_copy(t, i):
        to = outer_peer(i)
        return pltpu.make_async_remote_copy(
            src_ref=m_buf.at[t, z], dst_ref=m_buf.at[t, z],
            send_sem=c_send.at[t, i], recv_sem=c_recv.at[t, i],
            device_id={"lat": to * group + s}, device_id_type=MESH,
        )

    def d_copy(t, i):
        to = inner_peer(i)
        return pltpu.make_async_remote_copy(
            src_ref=v_buf.at[t, :, block(to)],
            dst_ref=y_ref.at[pl.ds((s * steps + t) * outer, outer)],
            send_sem=d_send.at[t, i], recv_sem=d_recv.at[t, i],
            device_id={"lat": z * group + to}, device_id_type=MESH,
        )

    def own_in(t):
        return pltpu.make_async_copy(
            x_ref.at[pl.ds((s * steps + t) * outer, outer)], r_buf.at[t, :, block(s)],
            local_sem.at[0, t],
        )

    def own_out(t):
        return pltpu.make_async_copy(
            v_buf.at[t, :, block(s)], y_ref.at[pl.ds((s * steps + t) * outer, outer)],
            local_sem.at[1, t],
        )

    for t in range(steps):
        own_in(t).start()
    pl.semaphore_wait(barrier, group - 1 + outer - 1)
    for t in range(steps):
        for i in range(1, group):
            a_copy(t, i).start()

    lane = lax.broadcasted_iota(jnp.int32, (1, 2 * channels), 1)
    fwd_sign = jnp.where(lane < channels, 1.0, -1.0).astype(jnp.float32)
    width = 2 * channels

    def forward(t):
        own_in(t).wait()
        for i in range(1, group):
            a_copy(t, i).wait_recv()
        for first in range(0, outer, 2):
            many = min(2, outer - first)
            pair = jnp.concatenate([r_buf[t, first + u] for u in range(many)], axis=1)
            both = jnp.dot(fwd_ref[...], pair, preferred_element_type=jnp.float32)
            for u in range(many):
                part = both[:, u * width:(u + 1) * width]
                out = part[:kept] + pltpu.roll(part[kept:], channels, 1) * fwd_sign
                p_buf[t, first + u] = out.astype(jnp.bfloat16)
        for i in range(1, outer):
            b_copy(t, i).start()

    def middle(t):
        total = p_buf[t, z].astype(jnp.float32)
        for i in range(1, outer):
            b_copy(t, i).wait_recv()
        for i in range(1, outer):
            total = total + q_buf[t, outer_peer(i)].astype(jnp.float32)
        mixed = jnp.dot(
            total.astype(jnp.bfloat16), mix_ref[t], preferred_element_type=jnp.float32
        )
        m_buf[t, z] = mixed.astype(jnp.bfloat16)
        for i in range(1, outer):
            c_copy(t, i).start()

    def backward(t):
        for i in range(1, outer):
            c_copy(t, i).wait_recv()
        for first in range(0, outer, 2):
            many = min(2, outer - first)
            pair = jnp.concatenate([m_buf[t, first + u] for u in range(many)], axis=1)
            both = jnp.dot(bwd_ref[...], pair, preferred_element_type=jnp.float32)
            for u in range(many):
                part = both[:, u * width:(u + 1) * width]
                out = part[:rows_all] - pltpu.roll(part[rows_all:], channels, 1) * fwd_sign
                v_buf[t, first + u] = out.astype(jnp.bfloat16)
        for i in range(1, group):
            d_copy(t, i).start()
        own_out(t).start()

    for step in range(steps + 2):
        if step < steps:
            forward(step)
        if 0 <= step - 1 < steps:
            middle(step - 1)
        if 0 <= step - 2 < steps:
            backward(step - 2)

    for t in range(steps):
        own_out(t).wait()
        for i in range(1, group):
            d_copy(t, i).wait()
            a_copy(t, i).wait_send()
        for i in range(1, outer):
            b_copy(t, i).wait_send()
            c_copy(t, i).wait_send()


def lat_part(x, mixing, forward_lat, backward_lat, devices, group):
    modes, rows, width = x.shape
    outer = devices // group
    steps = modes // devices
    kept = backward_lat.shape[1]
    dma = pltpu.SemaphoreType.DMA
    vmem = pl.BlockSpec(memory_space=pltpu.VMEM)
    return pl.pallas_call(
        functools.partial(lat_kernel, group, outer, steps, rows, kept, width // 2),
        out_shape=jax.ShapeDtypeStruct(x.shape, jnp.bfloat16),
        in_specs=[vmem] * 4,
        out_specs=vmem,
        scratch_shapes=[
            pltpu.VMEM((steps, outer, rows * group, width), jnp.bfloat16),
            pltpu.VMEM((steps, outer, kept, width), jnp.bfloat16),
            pltpu.VMEM((steps, outer, kept, width), jnp.bfloat16),
            pltpu.VMEM((steps, outer, kept, width), jnp.bfloat16),
            pltpu.VMEM((steps, outer, rows * group, width), jnp.bfloat16),
            dma((2, steps)),
            dma((steps, group)), dma((steps, group)),
            dma((steps, outer)), dma((steps, outer)),
            dma((steps, outer)), dma((steps, outer)),
            dma((steps, group)), dma((steps, group)),
        ],
        compiler_params=pltpu.CompilerParams(collective_id=0, has_side_effects=True),
        name="lat_part",
    )(x, mixing, forward_lat, backward_lat)


def mix_matrix(weight, channels):
    real_w = weight[..., :channels]
    imag_w = weight[..., channels:]
    lower = jnp.concatenate([-imag_w, real_w], axis=-1)
    return jnp.concatenate([weight, lower], axis=-2)


def shards(fields, spectral_weight, local_weight):
    row_count, channels, lon_count = fields.shape
    layer_count, mode_rows = spectral_weight.shape[:2]
    devices = lax.axis_size("lat")
    me = lax.axis_index("lat")
    group = math.gcd(devices, 8)
    outer = devices // group
    steps = mode_rows // devices
    table = lon_table(lon_count, mode_rows)
    forward_lon = jnp.asarray(table / math.sqrt(lon_count), jnp.bfloat16)
    backward_lon = jnp.asarray(
        table.transpose(2, 1, 0) / math.sqrt(mode_rows), jnp.bfloat16
    )
    forward_all, backward_all = lat_tables(devices, group, row_count, KY)
    forward_lat = lax.dynamic_index_in_dim(
        jnp.asarray(forward_all, jnp.bfloat16), me // group, 0, keepdims=False
    )
    backward_lat = lax.dynamic_index_in_dim(
        jnp.asarray(backward_all, jnp.bfloat16), me // group, 0, keepdims=False
    )
    grouped = spectral_weight.reshape(
        layer_count, group, steps, outer, channels, 2 * channels
    )
    grouped = lax.dynamic_index_in_dim(grouped, me % group, 1, keepdims=False)
    grouped = lax.dynamic_index_in_dim(grouped, me // group, 2, keepdims=False)
    mixing = mix_matrix(grouped, channels)
    current = fields
    for layer_idx in range(layer_count):
        x = jnp.einsum(
            "rcl,lpk->krpc", current, forward_lon, preferred_element_type=jnp.float32
        ).astype(jnp.bfloat16).reshape(mode_rows, row_count, 2 * channels)
        y = lat_part(x, mixing[layer_idx], forward_lat, backward_lat, devices, group)
        spectral = jnp.einsum(
            "krpc,kpl->rcl", y.reshape(mode_rows, row_count, 2, channels), backward_lon,
            preferred_element_type=jnp.float32,
        )
        pointwise = jnp.einsum(
            "rcl,cd->rdl", current, local_weight[layer_idx], preferred_element_type=jnp.float32
        )
        current = jax.nn.gelu(spectral + pointwise, approximate=True).astype(jnp.bfloat16)
    return current


def solution(mesh):
    return jax.shard_map(
        shards,
        mesh=mesh,
        in_specs=(P(("grp", "lat"), None, None), P(), P()),
        out_specs=P(("grp", "lat"), None, None),
        check_vma=False,
    )
```

time: 145 us -> 125 us (0.86)
  Pallas kernels: 0 us -> 84.2 us
  waiting for transfers between devices: 33.8 us -> 0 us
  other arithmetic: 25.3 us -> 0.22 us
  matrix products: 47.2 us -> 27.3 us
  starting transfers between devices: 18.6 us -> 0 us
  local copies, waits for them, and re-layouts: 18.9 us -> 13.2 us
    pallas_call x0 -> x2, Pallas kernels: none -> 84.2 us  [lat_part(): pl.pallas_call(functools.partial(lat_kernel, group, outer, steps, rows, k...]
    all_to_all x4 -> x0, waiting for transfers between devices: 33.8 us -> none  [the longest x2 17.2 us: shards(): lax.all_to_all(rebuilt, 'lat', split_axis=0, concat_axis=1, tiled=True)]
    all_to_all x4 -> x0, starting transfers between devices: 18.6 us -> none  [the longest x2 11 us: shards(): lax.all_to_all(lon_modes, 'lat', split_axis=1, concat_axis=0, tiled=True)]
    dot_general x8 -> x4, matrix products: 28.9 us -> 18.1 us  [the longest x2 11.3 us: shards(): jnp.einsum('krpc,kpl->rcl', y.reshape(mode_rows, row_count, 2, channels),...]
    another operation x2 -> x0, other arithmetic: 9.78 us -> none
    slice x2 -> x0, other arithmetic: 9.35 us -> none  [mix_matrix(): real_w = weight[..., :channels]]
    dot_general x2, matrix products: 18.2 us -> 9.22 us  [shards(): jnp.einsum('rcl,cd->rdl', current, local_weight[layer_idx], preferred_ele...]
    squeeze x0 -> x4, local copies, waits for them, and re-layouts: none -> 4.74 us  [the longest x1 1.57 us: shards(): lax.dynamic_index_in_dim(jnp.asarray(forward_all, jnp.bfloat16), me // gr...]
  transfers between devices with their start and end apart: 4 -> 0, of which waited for: 4 -> 0; matrix products, arithmetic and copies ran while one was open for 33% -> 0% of each run, Pallas kernels for 0% -> 0%
where the time goes in v1:
time: 125 us
  Pallas kernels  84.2 us (67%)
  matrix products  27.3 us (22%)
  local copies, waits for them, and re-layouts  13.2 us (11%)
    pallas_call x2, Pallas kernels, lat_part(): pl.pallas_call(functools.partial(lat_kernel, group, outer, steps, rows, k...  84.2 us
    dot_general x2, matrix products, shards(): jnp.einsum('krpc,kpl->rcl', y.reshape(mode_rows, row_count, 2, channels),...  11.3 us
    dot_general x2, matrix products, shards(): jnp.einsum('rcl,cd->rdl', current, local_weight[layer_idx], preferred_ele...  9.22 us
    dot_general x2, matrix products, shards(): jnp.einsum('rcl,lpk->krpc', current, forward_lon, preferred_element_type=...  6.78 us
    pallas_call x2, local copies, waits for them, and re-layouts, lat_part(): pl.pallas_call(functools.partial(lat_kernel, group, outer, steps, rows, k...  3.19 us
    unnamed x8, local copies, waits for them, and re-layouts  2.72 us
    reshape x2, local copies, waits for them, and re-layouts, shards(): x = jnp.einsum('rcl,lpk->krpc', current, forward_lon, preferred_element_t...  2.53 us

profile of v1, /device:TPU:0, one launch (start us, length us, event | category | flops | bytes accessed | tf_op | source)
XLA Modules:
  0.0 125.1 jit_solution(5959090623130840038)
XLA Ops:
  0.0 1.5 %dynamic-slice_bitcast_fusion.2.bwd_ref = bf16[384,128]{1,0:T(8,128)(2,1)} fusion(bf16[4,384,128]{2,1,0:T(8,128)(2,1)} %constant.98.clone, s32[]{:T(128)S(6)} %select_n.33), kind=kLoop, calls=%fused_computation.33 | loop fusion | bytes 196612 | tf_op jit(solution)/shard_map/jit(dynamic_index_in_dim)/squeeze | solution.py:238
  1.5 0.0 copy-start.1
  1.5 0.9 dynamic-slice_bitcast_fusion.1
  2.5 1.6 %dynamic-slice_bitcast_fusion.fwd_ref = bf16[256,192]{1,0:T(8,128)(2,1)} fusion(bf16[4,256,192]{2,1,0:T(8,128)(2,1)} %constant.97.clone, s32[]{:T(128)S(6)} %select_n.33), kind=kLoop, calls=%fused_computation.31 | loop fusion | bytes 196612 | tf_op jit(solution)/shard_map/jit(dynamic_index_in_dim)/squeeze | solution.py:235
  4.0 0.1 slice_negate_fusion
  4.1 0.1 maximum_maximum_fusion
  4.3 0.7 slice_bitcast_fusion
  5.0 4.9 %fusion.26 = bf16[128,24,2,64]{0,3,1,2:T(8,128)(2,1)S(1)} fusion(bf16[2048,2,128,1]{2,0,3,1:T(8,128)(2,1)} %constant.100, bf16[24,64,2048]{2,1,0:T(8,128)(2,1)} %param.7), kind=kOutput, calls=%fused_computation.26 | convolution fusion | flops 1611005952 | bytes 8126464 | tf_op jit(solution)/shard_map/rcl,lpk->krpc/dot_general | solution.py:249
  9.9 0.0 copy-start.2
  9.9 0.1 copy.15
  10.0 1.3 %copy.17.x_ref = bf16[128,24,128]{2,1,0:T(8,128)(2,1)} copy(bf16[128,24,128]{0,2,1:T(8,128)(2,1)S(1)} %bitcast.71) | data formatting | bytes 1572864 | tf_op jit(solution)/shard_map/reshape | solution.py:251
  11.2 43.5 %lat_part.2 = bf16[128,24,128]{2,1,0:T(8,128)(2,1)} custom-call(bf16[128,24,128]{2,1,0:T(8,128)(2,1)} %copy.17.x_ref, bf16[4,128,128]{2,1,0:T(8,128)(2,1)} %get-tuple-element.6.mix_ref, bf16[256,192]{1,0:T(8,128)(2,1)} %dynamic-slice_bitcast_fusion.fwd_ref, bf16[384,128]{1,0:T(8,128)(2,1)} %dynamic-slice_bitcast_fusion.2.bwd_ref), custom_call_target="tpu_custom_call" | custom-call | tf_op jit(solution)/shard_map/lat_part/pallas_call | solution.py:192
  54.7 1.6 %copy.18 = bf16[128,24,128]{0,2,1:T(8,128)(2,1)S(1)} copy(bf16[128,24,128]{2,1,0:T(8,128)(2,1)} %lat_part.2) | data formatting | bytes 1572864 | tf_op jit(solution)/shard_map/lat_part/pallas_call | solution.py:192
  56.3 0.0 copy-done.1
  56.3 4.6 %fusion.31 = f32[64,24,2048]{2,0,1:T(8,128)S(1)} fusion(bf16[24,64,2048]{2,1,0:T(8,128)(2,1)} %param.7, bf16[2,64,64]{2,1,0:T(8,128)(2,1)S(1)} %copy-done.1), kind=kOutput, calls=%fused_computation.36 | convolution fusion | flops 402653184 | bytes 18890752 | tf_op jit(solution)/shard_map/rcl,cd->rdl/dot_general | solution.py:257
  61.0 0.0 copy-done.2
  61.0 0.0 copy-start.3
  61.0 4.8 %fusion.7 = bf16[24,64,2048]{2,1,0:T(8,128)(2,1)S(1)} fusion(f32[64,24,2048]{2,0,1:T(8,128)S(1)} %fusion.31, bf16[128,24,2,64]{0,3,2,1:T(8,128)(2,1)S(1)} %bitcast.73, bf16[128,2,2048,1]{2,0,1,3:T(8,128)(2,1)S(1)} %copy-done.2), kind=kOutput, calls=%fused_computation.9 | convolution fusion | flops 1642070016 | bytes 20709376 | tf_op jit(solution)/shard_map/krpc,kpl->rcl/dot_general | solution.py:253
  65.8 0.0 copy-start
  65.8 2.7 %copy-done = bf16[24,64,2048]{2,1,0:T(8,128)(2,1)} copy-done((bf16[24,64,2048]{2,1,0:T(8,128)(2,1)}, bf16[24,64,2048]{2,1,0:T(8,128)(2,1)S(1)}, u32[]{:S(2)}) %copy-start) | copy-done | bytes 6291480
  68.5 0.0 copy-done.3
  68.5 1.9 %fusion.23 = bf16[24,64,2,128]{3,1,2,0:T(8,128)(2,1)S(1)} fusion(bf16[2048,2,128,1]{2,0,1,3:T(8,128)(2,1)S(1)} %copy-done.3, bf16[24,64,2048]{2,1,0:T(8,128)(2,1)S(1)} %fusion.7), kind=kOutput, calls=%fused_computation.25 | convolution fusion | flops 1611005952 | bytes 8126464 | tf_op jit(solution)/shard_map/rcl,lpk->krpc/dot_general | solution.py:249
  70.4 1.3 %copy.20.x_ref = bf16[128,24,128]{2,1,0:T(8,128)(2,1)} copy(bf16[128,24,128]{0,2,1:T(8,128)(2,1)S(1)} %bitcast.74) | data formatting | bytes 1572864 | tf_op jit(solution)/shard_map/reshape | solution.py:251
  71.7 40.7 %lat_part.3 = bf16[128,24,128]{2,1,0:T(8,128)(2,1)} custom-call(bf16[128,24,128]{2,1,0:T(8,128)(2,1)} %copy.20.x_ref, bf16[4,128,128]{2,1,0:T(8,128)(2,1)} %get-tuple-element.5.mix_ref, bf16[256,192]{1,0:T(8,128)(2,1)} %dynamic-slice_bitcast_fusion.fwd_ref, bf16[384,128]{1,0:T(8,128)(2,1)} %dynamic-slice_bitcast_fusion.2.bwd_ref), custom_call_target="tpu_custom_call" | custom-call | tf_op jit(solution)/shard_map/lat_part/pallas_call | solution.py:192
  112.4 1.6 %copy.21 = bf16[128,24,128]{0,2,1:T(8,128)(2,1)S(1)} copy(bf16[128,24,128]{2,1,0:T(8,128)(2,1)} %lat_part.3) | data formatting | bytes 1572864 | tf_op jit(solution)/shard_map/lat_part/pallas_call | solution.py:192
  114.0 4.6 %fusion.29 = f32[24,2048,64]{1,2,0:T(8,128)S(1)} fusion(bf16[24,64,2048]{2,1,0:T(8,128)(2,1)} %copy-done, bf16[2,64,64]{2,1,0:T(8,128)(2,1)S(1)} %copy-done.1), kind=kOutput, calls=%fused_computation.34 | convolution fusion | flops 402653184 | bytes 18890752 | tf_op jit(solution)/shard_map/rcl,cd->rdl/dot_general | solution.py:257
  118.6 6.5 %fusion.15 = bf16[24,64,2048]{2,1,0:T(8,128)(2,1)} fusion(f32[24,2048,64]{1,2,0:T(8,128)S(1)} %fusion.29, bf16[128,24,2,64]{0,3,2,1:T(8,128)(2,1)S(1)} %bitcast.72, bf16[128,2,2048,1]{2,0,1,3:T(8,128)(2,1)S(1)} %copy-done.2), kind=kOutput, calls=%fused_computation.17 | convolution fusion | flops 1642070016 | bytes 20709376 | tf_op jit(solution)/shard_map/krpc,kpl->rcl/dot_general | solution.py:253
Async XLA Ops:
  1.5 54.8 %copy-start.1 = (bf16[2,64,64]{2,1,0:T(8,128)(2,1)S(1)}, bf16[2,64,64]{2,1,0:T(8,128)(2,1)}, u32[]{:S(2)}) copy-start(bf16[2,64,64]{2,1,0:T(8,128)(2,1)} %param.9) | copy-start | bytes 49156
  9.9 51.1 %copy-start.2 = (bf16[128,2,2048,1]{2,0,1,3:T(8,128)(2,1)S(1)}, bf16[128,2,2048,1]{2,0,1,3:T(8,128)(2,1)}, u32[]{:S(2)}) copy-start(bf16[128,2,2048,1]{2,0,1,3:T(8,128)(2,1)} %constant.101) | copy-start | bytes 3145732
  61.0 7.5 %copy-start.3 = (bf16[2048,2,128,1]{2,0,1,3:T(8,128)(2,1)S(1)}, bf16[2048,2,128,1]{2,0,1,3:T(8,128)(2,1)}, u32[]{:S(2)}) copy-start(bf16[2048,2,128,1]{2,0,1,3:T(8,128)(2,1)} %constant.102) | copy-start | bytes 3145732
  65.8 2.7 %copy-start = (bf16[24,64,2048]{2,1,0:T(8,128)(2,1)}, bf16[24,64,2048]{2,1,0:T(8,128)(2,1)S(1)}, u32[]{:S(2)}) copy-start(bf16[24,64,2048]{2,1,0:T(8,128)(2,1)S(1)} %fusion.7) | copy-start | bytes 18874372

commit v2 on v1

--- a/solution.py
+++ b/solution.py
@@ -11,6 +11,8 @@
 
 KY = 128
 MESH = pl.DeviceIdType.MESH
+LAG = (0, 1, 2, 3, 4)
+ROW_BLOCK = 8
 
 
 def lon_table(lon_count, mode_count):
@@ -37,7 +39,7 @@
 def lat_kernel(
     group, outer, steps, rows, kept, channels,
     x_ref, mix_ref, fwd_ref, bwd_ref, y_ref,
-    r_buf, p_buf, q_buf, m_buf, v_buf,
+    r_buf, p_buf, q_buf, m_buf, v_buf, fwd_buf, bwd_buf, f_buf, acc, f_sem, g_sem,
     local_sem, a_send, a_recv, b_send, b_recv, c_send, c_recv, d_send, d_recv,
 ):
     me = lax.axis_index("lat")
@@ -110,12 +112,38 @@
             local_sem.at[1, t],
         )
 
+    def f_copy(t):
+        return pltpu.make_async_remote_copy(
+            src_ref=p_buf.at[t, outer - 1 - z], dst_ref=f_buf.at[t],
+            send_sem=f_sem.at[0, t], recv_sem=f_sem.at[1, t],
+            device_id={"lat": jnp.where(z == 0, 1, outer - 2) * group + s}, device_id_type=MESH,
+        )
+
+    def g_copy(t):
+        block_of = outer_peer(2)
+        return pltpu.make_async_remote_copy(
+            src_ref=m_buf.at[t, block_of], dst_ref=m_buf.at[t, block_of],
+            send_sem=g_sem.at[0, t], recv_sem=g_sem.at[1, t],
+            device_id={"lat": (outer - 1 - block_of) * group + s}, device_id_type=MESH,
+        )
+
+    relay = outer == 4
+    last = outer - 1
+    at_end = jnp.logical_or(z == 0, z == last)
+    inside = jnp.logical_not(at_end)
+
+    fwd_copy = pltpu.make_async_copy(fwd_ref.at[z], fwd_buf, local_sem.at[0, steps])
+    bwd_copy = pltpu.make_async_copy(bwd_ref.at[z], bwd_buf, local_sem.at[1, steps])
+    fwd_copy.start()
+    bwd_copy.start()
     for t in range(steps):
         own_in(t).start()
     pl.semaphore_wait(barrier, group - 1 + outer - 1)
     for t in range(steps):
         for i in range(1, group):
             a_copy(t, i).start()
+    fwd_copy.wait()
+    bwd_copy.wait()
 
     lane = lax.broadcasted_iota(jnp.int32, (1, 2 * channels), 1)
     fwd_sign = jnp.where(lane < channels, 1.0, -1.0).astype(jnp.float32)
@@ -128,34 +156,80 @@
         for first in range(0, outer, 2):
             many = min(2, outer - first)
             pair = jnp.concatenate([r_buf[t, first + u] for u in range(many)], axis=1)
-            both = jnp.dot(fwd_ref[...], pair, preferred_element_type=jnp.float32)
+            both = jnp.dot(fwd_buf[...], pair, preferred_element_type=jnp.float32)
             for u in range(many):
                 part = both[:, u * width:(u + 1) * width]
                 out = part[:kept] + pltpu.roll(part[kept:], channels, 1) * fwd_sign
                 p_buf[t, first + u] = out.astype(jnp.bfloat16)
-        for i in range(1, outer):
-            b_copy(t, i).start()
+        if not relay:
+            for i in range(1, outer):
+                b_copy(t, i).start()
+            return
+        pl.when(at_end)(lambda: f_copy(t).start())
+        pl.when(at_end)(lambda: b_copy(t, 2).start())
+        pl.when(z != last)(lambda: b_copy(t, 1).start())
+        pl.when(z != 0)(lambda: b_copy(t, last).start())
+
+    def relay_sum(t):
+        if not relay:
+            return
+
+        @pl.when(inside)
+        def _():
+            f_copy(t).wait_recv()
+            to = outer_peer(2)
+            p_buf[t, to] = (
+                p_buf[t, to].astype(jnp.float32) + f_buf[t].astype(jnp.float32)
+            ).astype(jnp.bfloat16)
+            b_copy(t, 2).start()
+
+    def collect(t, i):
+        b_copy(t, i).wait_recv()
+        acc[...] += q_buf[t, lax.rem(z + outer - i, outer)].astype(jnp.float32)
 
     def middle(t):
-        total = p_buf[t, z].astype(jnp.float32)
-        for i in range(1, outer):
-            b_copy(t, i).wait_recv()
-        for i in range(1, outer):
-            total = total + q_buf[t, outer_peer(i)].astype(jnp.float32)
+        acc[...] = p_buf[t, z].astype(jnp.float32)
+        if relay:
+            pl.when(z != 0)(lambda: collect(t, 1))
+            pl.when(z != last)(lambda: collect(t, last))
+            collect(t, 2)
+        else:
+            for i in range(1, outer):
+                collect(t, i)
         mixed = jnp.dot(
-            total.astype(jnp.bfloat16), mix_ref[t], preferred_element_type=jnp.float32
+            acc[...].astype(jnp.bfloat16), mix_ref[t], preferred_element_type=jnp.float32
         )
         m_buf[t, z] = mixed.astype(jnp.bfloat16)
-        for i in range(1, outer):
-            c_copy(t, i).start()
+        if relay:
+            c_copy(t, 2).start()
+            pl.when(z != last)(lambda: c_copy(t, 1).start())
+            pl.when(z != 0)(lambda: c_copy(t, last).start())
+        else:
+            for i in range(1, outer):
+                c_copy(t, i).start()
+
+    def relay_out(t):
+        if not relay:
+            return
+
+        @pl.when(inside)
+        def _():
+            c_copy(t, 2).wait_recv()
+            g_copy(t).start()
 
     def backward(t):
-        for i in range(1, outer):
-            c_copy(t, i).wait_recv()
+        if relay:
+            pl.when(z != 0)(lambda: c_copy(t, 1).wait_recv())
+            pl.when(z != last)(lambda: c_copy(t, last).wait_recv())
+            pl.when(at_end)(lambda: c_copy(t, 2).wait_recv())
+            pl.when(at_end)(lambda: g_copy(t).wait_recv())
+        else:
+            for i in range(1, outer):
+                c_copy(t, i).wait_recv()
         for first in range(0, outer, 2):
             many = min(2, outer - first)
             pair = jnp.concatenate([m_buf[t, first + u] for u in range(many)], axis=1)
-            both = jnp.dot(bwd_ref[...], pair, preferred_element_type=jnp.float32)
+            both = jnp.dot(bwd_buf[...], pair, preferred_element_type=jnp.float32)
             for u in range(many):
                 part = both[:, u * width:(u + 1) * width]
                 out = part[:rows_all] - pltpu.roll(part[rows_all:], channels, 1) * fwd_sign
@@ -164,35 +238,42 @@
             d_copy(t, i).start()
         own_out(t).start()
 
-    for step in range(steps + 2):
-        if step < steps:
-            forward(step)
-        if 0 <= step - 1 < steps:
-            middle(step - 1)
-        if 0 <= step - 2 < steps:
-            backward(step - 2)
+    stages = tuple(zip((forward, relay_sum, middle, relay_out, backward), LAG))
+    for step in range(steps + max(LAG)):
+        for stage, lag in stages:
+            if 0 <= step - lag < steps:
+                stage(step - lag)
 
     for t in range(steps):
         own_out(t).wait()
         for i in range(1, group):
             d_copy(t, i).wait()
             a_copy(t, i).wait_send()
-        for i in range(1, outer):
-            b_copy(t, i).wait_send()
-            c_copy(t, i).wait_send()
+        if relay:
+            pl.when(at_end)(lambda: f_copy(t).wait_send())
+            pl.when(inside)(lambda: g_copy(t).wait_send())
+            for copy in (b_copy, c_copy):
+                copy(t, 2).wait_send()
+                pl.when(z != last)(lambda: copy(t, 1).wait_send())
+                pl.when(z != 0)(lambda: copy(t, last).wait_send())
+        else:
+            for i in range(1, outer):
+                b_copy(t, i).wait_send()
+                c_copy(t, i).wait_send()
 
 
 def lat_part(x, mixing, forward_lat, backward_lat, devices, group):
     modes, rows, width = x.shape
     outer = devices // group
     steps = modes // devices
-    kept = backward_lat.shape[1]
+    kept = backward_lat.shape[2]
     dma = pltpu.SemaphoreType.DMA
     vmem = pl.BlockSpec(memory_space=pltpu.VMEM)
+    hbm = pl.BlockSpec(memory_space=pl.ANY)
     return pl.pallas_call(
         functools.partial(lat_kernel, group, outer, steps, rows, kept, width // 2),
         out_shape=jax.ShapeDtypeStruct(x.shape, jnp.bfloat16),
-        in_specs=[vmem] * 4,
+        in_specs=[vmem, vmem, hbm, hbm],
         out_specs=vmem,
         scratch_shapes=[
             pltpu.VMEM((steps, outer, rows * group, width), jnp.bfloat16),
@@ -200,7 +281,12 @@
             pltpu.VMEM((steps, outer, kept, width), jnp.bfloat16),
             pltpu.VMEM((steps, outer, kept, width), jnp.bfloat16),
             pltpu.VMEM((steps, outer, rows * group, width), jnp.bfloat16),
-            dma((2, steps)),
+            pltpu.VMEM(forward_lat.shape[1:], jnp.bfloat16),
+            pltpu.VMEM(backward_lat.shape[1:], jnp.bfloat16),
+            pltpu.VMEM((steps, kept, width), jnp.bfloat16),
+            pltpu.VMEM((kept, width), jnp.float32),
+            dma((2, steps)), dma((2, steps)),
+            dma((2, steps + 1)),
             dma((steps, group)), dma((steps, group)),
             dma((steps, outer)), dma((steps, outer)),
             dma((steps, outer)), dma((steps, outer)),
@@ -209,6 +295,112 @@
         compiler_params=pltpu.CompilerParams(collective_id=0, has_side_effects=True),
         name="lat_part",
     )(x, mixing, forward_lat, backward_lat)
+
+
+def modes_out(flat, x_ref, turn):
+    modes, rows, width = x_ref.shape
+    channels = width // 2
+    for n in range(rows):
+        part = flat[n * channels:(n + 1) * channels]
+        stacked = jnp.concatenate([part[:, :modes], part[:, modes:]], axis=0)
+        turn[pl.ds(n, modes, stride=rows), :] = stacked.T
+    x_ref[...] = turn[...].reshape(modes, rows, width).astype(jnp.bfloat16)
+
+
+def lon_kernel(h_ref, table_ref, x_ref, turn):
+    rows, channels, lon_count = h_ref.shape
+    flat = jnp.dot(
+        h_ref[...].reshape(rows * channels, lon_count), table_ref[...],
+        preferred_element_type=jnp.float32,
+    )
+    modes_out(flat, x_ref, turn)
+
+
+def field_kernel(with_modes, y_ref, h_ref, back_ref, local_ref, *rest):
+    if with_modes:
+        table_ref, out_ref, x_ref, turn, turned = rest
+    else:
+        out_ref, turn, turned = rest
+    modes, rows, width = y_ref.shape
+    channels = width // 2
+    lon_count = h_ref.shape[2]
+    span = local_ref.shape[0] // channels
+    turn[...] = y_ref[...].astype(jnp.float32).reshape(modes * rows, width)
+    for n in range(rows):
+        across = turn[pl.ds(n, modes, stride=rows), :].T
+        turned[n * channels:(n + 1) * channels] = jnp.concatenate(
+            [across[:channels], across[channels:]], axis=1
+        ).astype(jnp.bfloat16)
+    chunk = min(512, lon_count)
+    inner = math.sqrt(2.0 / math.pi)
+    for first in range(0, rows, span):
+        many = span * channels
+        spectrum = turned[first * channels:first * channels + many]
+        for column in range(0, lon_count, chunk):
+            cells = slice(column, column + chunk)
+            total = jnp.dot(
+                spectrum, back_ref[:, cells], preferred_element_type=jnp.float32
+            ) + jnp.dot(
+                local_ref[...], h_ref[first:first + span, :, cells].reshape(many, chunk),
+                preferred_element_type=jnp.float32,
+            )
+            curve = jnp.tanh(total * (inner + (inner * 0.044715) * (total * total)))
+            out_ref[first:first + span, :, cells] = (
+                (total * (0.5 + 0.5 * curve)).astype(jnp.bfloat16).reshape(span, channels, chunk)
+            )
+    if with_modes:
+        flat = jnp.dot(
+            out_ref[...].reshape(rows * channels, lon_count), table_ref[...],
+            preferred_element_type=jnp.float32,
+        )
+        modes_out(flat, x_ref, turn)
+
+
+def whole_block(array):
+    return pl.BlockSpec(array.shape, lambda i: (0,) * array.ndim, pipeline_mode=pl.Buffered(1))
+
+
+def lon_part(h, table):
+    rows, channels, lon_count = h.shape
+    modes = table.shape[1] // 2
+    width = 2 * channels
+    return pl.pallas_call(
+        lon_kernel,
+        grid=(rows // ROW_BLOCK,),
+        out_shape=jax.ShapeDtypeStruct((modes, rows, width), jnp.bfloat16),
+        in_specs=[
+            pl.BlockSpec((ROW_BLOCK, channels, lon_count), lambda i: (i, 0, 0)),
+            whole_block(table),
+        ],
+        out_specs=pl.BlockSpec((modes, ROW_BLOCK, width), lambda i: (0, i, 0)),
+        scratch_shapes=[pltpu.VMEM((modes * ROW_BLOCK, width), jnp.float32)],
+        name="lon_part",
+    )(h, table)
+
+
+def field_part(y, h, back, local, table=None):
+    rows, channels, lon_count = h.shape
+    modes, _, width = y.shape
+    field = pl.BlockSpec((ROW_BLOCK, channels, lon_count), lambda i: (i, 0, 0))
+    spectral = pl.BlockSpec((modes, ROW_BLOCK, width), lambda i: (0, i, 0))
+    with_modes = table is not None
+    operands = [y, h, back, local] + ([table] if with_modes else [])
+    shapes = [jax.ShapeDtypeStruct(h.shape, jnp.bfloat16)]
+    if with_modes:
+        shapes.append(jax.ShapeDtypeStruct(y.shape, jnp.bfloat16))
+    out = pl.pallas_call(
+        functools.partial(field_kernel, with_modes),
+        grid=(rows // ROW_BLOCK,),
+        out_shape=shapes,
+        in_specs=[spectral, field] + [whole_block(a) for a in operands[2:]],
+        out_specs=[field, spectral][:len(shapes)],
+        scratch_shapes=[
+            pltpu.VMEM((modes * ROW_BLOCK, width), jnp.float32),
+            pltpu.VMEM((ROW_BLOCK * channels, 2 * modes), jnp.bfloat16),
+        ],
+        name="field_part",
+    )(*operands)
+    return (out[0], out[1]) if with_modes else (out[0], None)
 
 
 def mix_matrix(weight, channels):
@@ -227,17 +419,20 @@
     outer = devices // group
     steps = mode_rows // devices
     table = lon_table(lon_count, mode_rows)
-    forward_lon = jnp.asarray(table / math.sqrt(lon_count), jnp.bfloat16)
+    forward_lon = jnp.asarray(
+        (table / math.sqrt(lon_count)).reshape(lon_count, 2 * mode_rows), jnp.bfloat16
+    )
     backward_lon = jnp.asarray(
-        table.transpose(2, 1, 0) / math.sqrt(mode_rows), jnp.bfloat16
+        (table.transpose(1, 2, 0) / math.sqrt(mode_rows)).reshape(2 * mode_rows, lon_count),
+        jnp.bfloat16,
     )
+    span = max(1, min(ROW_BLOCK, 256 // channels))
+    local = jnp.einsum(
+        "ab,lcd->ladbc", jnp.eye(span, dtype=jnp.bfloat16), local_weight
+    ).reshape(layer_count, span * channels, span * channels)
     forward_all, backward_all = lat_tables(devices, group, row_count, KY)
-    forward_lat = lax.dynamic_index_in_dim(
-        jnp.asarray(forward_all, jnp.bfloat16), me // group, 0, keepdims=False
-    )
-    backward_lat = lax.dynamic_index_in_dim(
-        jnp.asarray(backward_all, jnp.bfloat16), me // group, 0, keepdims=False
-    )
+    forward_lat = jnp.asarray(forward_all, jnp.bfloat16)
+    backward_lat = jnp.asarray(backward_all, jnp.bfloat16)
     grouped = spectral_weight.reshape(
         layer_count, group, steps, outer, channels, 2 * channels
     )
@@ -245,19 +440,13 @@
     grouped = lax.dynamic_index_in_dim(grouped, me // group, 2, keepdims=False)
     mixing = mix_matrix(grouped, channels)
     current = fields
+    x = lon_part(current, forward_lon)
     for layer_idx in range(layer_count):
-        x = jnp.einsum(
-            "rcl,lpk->krpc", current, forward_lon, preferred_element_type=jnp.float32
-        ).astype(jnp.bfloat16).reshape(mode_rows, row_count, 2 * channels)
         y = lat_part(x, mixing[layer_idx], forward_lat, backward_lat, devices, group)
-        spectral = jnp.einsum(
-            "krpc,kpl->rcl", y.reshape(mode_rows, row_count, 2, channels), backward_lon,
-            preferred_element_type=jnp.float32,
-        )
-        pointwise = jnp.einsum(
-            "rcl,cd->rdl", current, local_weight[layer_idx], preferred_element_type=jnp.float32
-        )
-        current = jax.nn.gelu(spectral + pointwise, approximate=True).astype(jnp.bfloat16)
+        last_layer = layer_idx == layer_count - 1
+        current, x = field_part(
+            y, current, backward_lon, local[layer_idx], None if last_layer else forward_lon
+        )
     return current
 
 

time: 125 us -> 112 us (0.90)
  matrix products: 27.3 us -> 0 us
  Pallas kernels: 84.2 us -> 106 us
  local copies, waits for them, and re-layouts: 13.2 us -> 4.42 us
    dot_general x6 -> x0, matrix products: 27.3 us -> none  [the longest x2 11.3 us: shards(): jnp.einsum('krpc,kpl->rcl', y.reshape(mode_rows, row_count, 2, channels),...]
    pallas_call x0 -> x3, Pallas kernels: none -> 26.1 us  [the longest x2 20.2 us: field_part(): pl.pallas_call(functools.partial(field_kernel, with_modes), grid=(rows //...]
    pallas_call x2, Pallas kernels: 84.2 us -> 80.1 us  [lat_part(): pl.pallas_call(functools.partial(lat_kernel, group, outer, steps, rows, k...]
    pallas_call x2 -> x0, local copies, waits for them, and re-layouts: 3.19 us -> none  [lat_part(): pl.pallas_call(functools.partial(lat_kernel, group, outer, steps, rows, k...]
    reshape x2 -> x0, local copies, waits for them, and re-layouts: 2.53 us -> none  [shards(): x = jnp.einsum('rcl,lpk->krpc', current, forward_lon, preferred_element_t...]
    unnamed x8 -> x1, local copies, waits for them, and re-layouts: 2.72 us -> 0.85 us
    squeeze x2, local copies, waits for them, and re-layouts: 3.1 us -> 1.73 us  [shards(): local[layer_idx]]
where the time goes in v2:
time: 112 us; the launch traced here: 111 us
  Pallas kernels  106 us (95%)
  local copies, waits for them, and re-layouts  4.42 us (4%)
    pallas_call x2, Pallas kernels, lat_part(): pl.pallas_call(functools.partial(lat_kernel, group, outer, steps, rows, k...  80.1 us
    pallas_call x2, Pallas kernels, field_part(): pl.pallas_call(functools.partial(field_kernel, with_modes), grid=(rows //...  20.2 us
    pallas_call x1, Pallas kernels, lon_part(): pl.pallas_call(lon_kernel, grid=(rows // ROW_BLOCK,), out_shape=jax.Shape...  5.9 us

profile of v2, /device:TPU:0, one launch (start us, length us, event | category | flops | bytes accessed | tf_op | source)
XLA Modules:
  0.0 111.2 jit_solution(7549896797397335075)
XLA Ops:
  0.0 0.8 copy.9
  0.9 0.9 dynamic-slice_bitcast_fusion
  1.8 0.1 slice_negate_fusion
  1.9 0.1 maximum_maximum_fusion
  2.0 0.7 slice_bitcast_fusion
  2.7 0.3 multiply_bitcast_fusion
  3.0 0.2 fusion.1
  3.2 0.9 squeeze.22.local_ref
  4.1 0.9 squeeze.20.local_ref
  4.9 5.9 %lon_part.1.x_ref = bf16[128,24,128]{2,1,0:T(8,128)(2,1)} custom-call(bf16[24,64,2048]{2,1,0:T(8,128)(2,1)} %h_ref.3, bf16[2048,256]{1,0:T(8,128)(2,1)} %constant.75.clone.table_ref.rest_0_), custom_call_target="tpu_custom_call" | custom-call | tf_op jit(solution)/shard_map/lon_part/pallas_call | solution.py:367
  10.8 41.7 %lat_part.2.y_ref = bf16[128,24,128]{2,1,0:T(8,128)(2,1)} custom-call(bf16[128,24,128]{2,1,0:T(8,128)(2,1)} %lon_part.1.x_ref, bf16[4,128,128]{2,1,0:T(8,128)(2,1)} %get-tuple-element.12.mix_ref, bf16[4,256,192]{2,1,0:T(8,128)(2,1)} %constant.77.clone.fwd_ref, bf16[4,384,128]{2,1,0:T(8,128)(2,1)} %constant.78.clone.bwd_ref), custom_call_target="tpu_custom_call" | custom-call | tf_op jit(solution)/shard_map/lat_part/pallas_call | solution.py:273
  52.5 10.7 %field_part.2 = (bf16[24,64,2048]{2,1,0:T(8,128)(2,1)}, bf16[128,24,128]{2,1,0:T(8,128)(2,1)}) custom-call(bf16[128,24,128]{2,1,0:T(8,128)(2,1)} %lat_part.2.y_ref, bf16[24,64,2048]{2,1,0:T(8,128)(2,1)} %h_ref.3, bf16[256,2048]{1,0:T(8,128)(2,1)} %constant.76.clone.back_ref, bf16[256,256]{1,0:T(8,128)(2,1)} %squeeze.20.local_ref, ...), custom_call_target="tpu_custom_call" | custom-call | tf_op jit(solution)/shard_map/field_part/pallas_call | solution.py:391
  63.2 38.4 %lat_part.3.y_ref = bf16[128,24,128]{2,1,0:T(8,128)(2,1)} custom-call(bf16[128,24,128]{2,1,0:T(8,128)(2,1)} %get-tuple-element.7.x_ref, bf16[4,128,128]{2,1,0:T(8,128)(2,1)} %get-tuple-element.11.mix_ref, bf16[4,256,192]{2,1,0:T(8,128)(2,1)} %constant.77.clone.fwd_ref, bf16[4,384,128]{2,1,0:T(8,128)(2,1)} %constant.78.clone.bwd_ref), custom_call_target="tpu_custom_call" | custom-call | tf_op jit(solution)/shard_map/lat_part/pallas_call | solution.py:273
  101.7 9.5 %field_part.3 = bf16[24,64,2048]{2,1,0:T(8,128)(2,1)} custom-call(bf16[128,24,128]{2,1,0:T(8,128)(2,1)} %lat_part.3.y_ref, bf16[24,64,2048]{2,1,0:T(8,128)(2,1)} %get-tuple-element.8.h_ref, bf16[256,2048]{1,0:T(8,128)(2,1)} %constant.76.clone.back_ref, bf16[256,256]{1,0:T(8,128)(2,1)} %squeeze.22.local_ref), custom_call_target="tpu_custom_call" | custom-call | tf_op jit(solution)/shard_map/field_part/pallas_call | solution.py:391
  (1 shorter events, 0.0 us)

commit v3 on v2

--- a/solution.py
+++ b/solution.py
@@ -13,6 +13,7 @@
 MESH = pl.DeviceIdType.MESH
 LAG = (0, 1, 2, 3, 4)
 ROW_BLOCK = 8
+CHUNK = 512
 
 
 def lon_table(lon_count, mode_count):
@@ -37,10 +38,10 @@
 
 
 def lat_kernel(
-    group, outer, steps, rows, kept, channels,
-    x_ref, mix_ref, fwd_ref, bwd_ref, y_ref,
-    r_buf, p_buf, q_buf, m_buf, v_buf, fwd_buf, bwd_buf, f_buf, acc, f_sem, g_sem,
-    local_sem, a_send, a_recv, b_send, b_recv, c_send, c_recv, d_send, d_recv,
+    layer, group, outer, steps, rows, kept, channels,
+    x_ref, weight_ref, fwd_ref, bwd_ref, y_ref,
+    r_buf, p_buf, q_buf, m_buf, v_buf, fwd_buf, bwd_buf, w_buf, mix_buf, f_buf, acc, f_sem, g_sem,
+    local_sem, w_sem, a_send, a_recv, b_send, b_recv, c_send, c_recv, d_send, d_recv,
 ):
     me = lax.axis_index("lat")
     z = me // group
@@ -134,8 +135,16 @@
 
     fwd_copy = pltpu.make_async_copy(fwd_ref.at[z], fwd_buf, local_sem.at[0, steps])
     bwd_copy = pltpu.make_async_copy(bwd_ref.at[z], bwd_buf, local_sem.at[1, steps])
+    w_copies = [
+        pltpu.make_async_copy(
+            weight_ref.at[layer, (s * steps + t) * outer + z], w_buf.at[t], w_sem.at[t]
+        )
+        for t in range(steps)
+    ]
     fwd_copy.start()
     bwd_copy.start()
+    for copy in w_copies:
+        copy.start()
     for t in range(steps):
         own_in(t).start()
     pl.semaphore_wait(barrier, group - 1 + outer - 1)
@@ -148,6 +157,13 @@
     lane = lax.broadcasted_iota(jnp.int32, (1, 2 * channels), 1)
     fwd_sign = jnp.where(lane < channels, 1.0, -1.0).astype(jnp.float32)
     width = 2 * channels
+    for t in range(steps):
+        w_copies[t].wait()
+        weight = w_buf[t].astype(jnp.float32)
+        mix_buf[t, :channels] = w_buf[t]
+        mix_buf[t, channels:] = (
+            pltpu.roll(weight, channels, 1) * -fwd_sign
+        ).astype(jnp.bfloat16)
 
     def forward(t):
         own_in(t).wait()
@@ -197,7 +213,7 @@
             for i in range(1, outer):
                 collect(t, i)
         mixed = jnp.dot(
-            acc[...].astype(jnp.bfloat16), mix_ref[t], preferred_element_type=jnp.float32
+            acc[...].astype(jnp.bfloat16), mix_buf[t], preferred_element_type=jnp.float32
         )
         m_buf[t, z] = mixed.astype(jnp.bfloat16)
         if relay:
@@ -262,7 +278,7 @@
                 c_copy(t, i).wait_send()
 
 
-def lat_part(x, mixing, forward_lat, backward_lat, devices, group):
+def lat_part(x, weight, layer, forward_lat, backward_lat, devices, group):
     modes, rows, width = x.shape
     outer = devices // group
     steps = modes // devices
@@ -271,9 +287,9 @@
     vmem = pl.BlockSpec(memory_space=pltpu.VMEM)
     hbm = pl.BlockSpec(memory_space=pl.ANY)
     return pl.pallas_call(
-        functools.partial(lat_kernel, group, outer, steps, rows, kept, width // 2),
+        functools.partial(lat_kernel, layer, group, outer, steps, rows, kept, width // 2),
         out_shape=jax.ShapeDtypeStruct(x.shape, jnp.bfloat16),
-        in_specs=[vmem, vmem, hbm, hbm],
+        in_specs=[vmem, hbm, hbm, hbm],
         out_specs=vmem,
         scratch_shapes=[
             pltpu.VMEM((steps, outer, rows * group, width), jnp.bfloat16),
@@ -283,18 +299,20 @@
             pltpu.VMEM((steps, outer, rows * group, width), jnp.bfloat16),
             pltpu.VMEM(forward_lat.shape[1:], jnp.bfloat16),
             pltpu.VMEM(backward_lat.shape[1:], jnp.bfloat16),
+            pltpu.VMEM((steps, width // 2, width), jnp.bfloat16),
+            pltpu.VMEM((steps, width, width), jnp.bfloat16),
             pltpu.VMEM((steps, kept, width), jnp.bfloat16),
             pltpu.VMEM((kept, width), jnp.float32),
             dma((2, steps)), dma((2, steps)),
-            dma((2, steps + 1)),
+            dma((2, steps + 1)), dma((steps,)),
             dma((steps, group)), dma((steps, group)),
             dma((steps, outer)), dma((steps, outer)),
             dma((steps, outer)), dma((steps, outer)),
             dma((steps, group)), dma((steps, group)),
         ],
-        compiler_params=pltpu.CompilerParams(collective_id=0, has_side_effects=True),
+        compiler_params=pltpu.CompilerParams(collective_id=layer, has_side_effects=True),
         name="lat_part",
-    )(x, mixing, forward_lat, backward_lat)
+    )(x, weight, forward_lat, backward_lat)
 
 
 def modes_out(flat, x_ref, turn):
@@ -316,22 +334,31 @@
     modes_out(flat, x_ref, turn)
 
 
-def field_kernel(with_modes, y_ref, h_ref, back_ref, local_ref, *rest):
+def field_kernel(layer, with_modes, y_ref, h_ref, back_ref, local_ref, *rest):
     if with_modes:
-        table_ref, out_ref, x_ref, turn, turned = rest
+        table_ref, out_ref, x_ref, turn, turned, pointwise = rest
     else:
-        out_ref, turn, turned = rest
+        out_ref, turn, turned, pointwise = rest
     modes, rows, width = y_ref.shape
     channels = width // 2
     lon_count = h_ref.shape[2]
-    span = local_ref.shape[0] // channels
+    span = pointwise.shape[0] // channels
+
+    @pl.when(pl.program_id(0) == 0)
+    def _():
+        pointwise[...] = jnp.zeros_like(pointwise)
+        mixing = local_ref[layer].astype(jnp.float32).T.astype(jnp.bfloat16)
+        for n in range(span):
+            own = slice(n * channels, (n + 1) * channels)
+            pointwise[own, own] = mixing
+
     turn[...] = y_ref[...].astype(jnp.float32).reshape(modes * rows, width)
     for n in range(rows):
         across = turn[pl.ds(n, modes, stride=rows), :].T
         turned[n * channels:(n + 1) * channels] = jnp.concatenate(
             [across[:channels], across[channels:]], axis=1
         ).astype(jnp.bfloat16)
-    chunk = min(512, lon_count)
+    chunk = min(CHUNK, lon_count)
     inner = math.sqrt(2.0 / math.pi)
     for first in range(0, rows, span):
         many = span * channels
@@ -341,7 +368,7 @@
             total = jnp.dot(
                 spectrum, back_ref[:, cells], preferred_element_type=jnp.float32
             ) + jnp.dot(
-                local_ref[...], h_ref[first:first + span, :, cells].reshape(many, chunk),
+                pointwise[...], h_ref[first:first + span, :, cells].reshape(many, chunk),
                 preferred_element_type=jnp.float32,
             )
             curve = jnp.tanh(total * (inner + (inner * 0.044715) * (total * total)))
@@ -378,18 +405,19 @@
     )(h, table)
 
 
-def field_part(y, h, back, local, table=None):
+def field_part(y, h, back, local, layer, table=None):
     rows, channels, lon_count = h.shape
     modes, _, width = y.shape
     field = pl.BlockSpec((ROW_BLOCK, channels, lon_count), lambda i: (i, 0, 0))
     spectral = pl.BlockSpec((modes, ROW_BLOCK, width), lambda i: (0, i, 0))
     with_modes = table is not None
+    many = max(1, min(ROW_BLOCK, 256 // channels)) * channels
     operands = [y, h, back, local] + ([table] if with_modes else [])
     shapes = [jax.ShapeDtypeStruct(h.shape, jnp.bfloat16)]
     if with_modes:
         shapes.append(jax.ShapeDtypeStruct(y.shape, jnp.bfloat16))
     out = pl.pallas_call(
-        functools.partial(field_kernel, with_modes),
+        functools.partial(field_kernel, layer, with_modes),
         grid=(rows // ROW_BLOCK,),
         out_shape=shapes,
         in_specs=[spectral, field] + [whole_block(a) for a in operands[2:]],
@@ -397,27 +425,18 @@
         scratch_shapes=[
             pltpu.VMEM((modes * ROW_BLOCK, width), jnp.float32),
             pltpu.VMEM((ROW_BLOCK * channels, 2 * modes), jnp.bfloat16),
+            pltpu.VMEM((many, many), jnp.bfloat16),
         ],
         name="field_part",
     )(*operands)
     return (out[0], out[1]) if with_modes else (out[0], None)
 
 
-def mix_matrix(weight, channels):
-    real_w = weight[..., :channels]
-    imag_w = weight[..., channels:]
-    lower = jnp.concatenate([-imag_w, real_w], axis=-1)
-    return jnp.concatenate([weight, lower], axis=-2)
-
-
 def shards(fields, spectral_weight, local_weight):
     row_count, channels, lon_count = fields.shape
     layer_count, mode_rows = spectral_weight.shape[:2]
     devices = lax.axis_size("lat")
-    me = lax.axis_index("lat")
     group = math.gcd(devices, 8)
-    outer = devices // group
-    steps = mode_rows // devices
     table = lon_table(lon_count, mode_rows)
     forward_lon = jnp.asarray(
         (table / math.sqrt(lon_count)).reshape(lon_count, 2 * mode_rows), jnp.bfloat16
@@ -426,26 +445,17 @@
         (table.transpose(1, 2, 0) / math.sqrt(mode_rows)).reshape(2 * mode_rows, lon_count),
         jnp.bfloat16,
     )
-    span = max(1, min(ROW_BLOCK, 256 // channels))
-    local = jnp.einsum(
-        "ab,lcd->ladbc", jnp.eye(span, dtype=jnp.bfloat16), local_weight
-    ).reshape(layer_count, span * channels, span * channels)
     forward_all, backward_all = lat_tables(devices, group, row_count, KY)
     forward_lat = jnp.asarray(forward_all, jnp.bfloat16)
     backward_lat = jnp.asarray(backward_all, jnp.bfloat16)
-    grouped = spectral_weight.reshape(
-        layer_count, group, steps, outer, channels, 2 * channels
-    )
-    grouped = lax.dynamic_index_in_dim(grouped, me % group, 1, keepdims=False)
-    grouped = lax.dynamic_index_in_dim(grouped, me // group, 2, keepdims=False)
-    mixing = mix_matrix(grouped, channels)
     current = fields
     x = lon_part(current, forward_lon)
     for layer_idx in range(layer_count):
-        y = lat_part(x, mixing[layer_idx], forward_lat, backward_lat, devices, group)
+        y = lat_part(x, spectral_weight, layer_idx, forward_lat, backward_lat, devices, group)
         last_layer = layer_idx == layer_count - 1
         current, x = field_part(
-            y, current, backward_lon, local[layer_idx], None if last_layer else forward_lon
+            y, current, backward_lon, local_weight, layer_idx,
+            None if last_layer else forward_lon,
         )
     return current
 

time: 112 us -> 107 us (0.955)
  local copies, waits for them, and re-layouts: 4.42 us -> 0 us
    squeeze x4 -> x0, local copies, waits for them, and re-layouts: 3.39 us -> none  [the longest x2 1.73 us: shards(): local[layer_idx]]
where the time goes in v3:
time: 107 us; the launch traced here: 106 us
  Pallas kernels  106 us (99%)
    pallas_call x2, Pallas kernels, lat_part(): pl.pallas_call(functools.partial(lat_kernel, layer, group, outer, steps,...  80.2 us
    pallas_call x2, Pallas kernels, field_part(): pl.pallas_call(functools.partial(field_kernel, layer, with_modes), grid=(...  20.2 us
    pallas_call x1, Pallas kernels, lon_part(): pl.pallas_call(lon_kernel, grid=(rows // ROW_BLOCK,), out_shape=jax.Shape...  5.9 us

profile of v3, /device:TPU:0, one launch (start us, length us, event | category | flops | bytes accessed | tf_op | source)
XLA Modules:
  0.0 106.4 jit_solution(14256199941523807398)
XLA Ops:
  0.0 5.9 %lon_part.1.x_ref = bf16[128,24,128]{2,1,0:T(8,128)(2,1)} custom-call(bf16[24,64,2048]{2,1,0:T(8,128)(2,1)} %h_ref.3, bf16[2048,256]{1,0:T(8,128)(2,1)} %constant.8.clone.table_ref.rest_0_), custom_call_target="tpu_custom_call" | custom-call | tf_op jit(solution)/shard_map/lon_part/pallas_call | solution.py:394
  5.9 41.7 %lat_part.2.y_ref = bf16[128,24,128]{2,1,0:T(8,128)(2,1)} custom-call(bf16[128,24,128]{2,1,0:T(8,128)(2,1)} %lon_part.1.x_ref, bf16[2,128,64,128]{3,2,1,0:T(8,128)(2,1)} %weight_ref.3, bf16[4,256,192]{2,1,0:T(8,128)(2,1)} %constant.10.clone.fwd_ref, bf16[4,384,128]{2,1,0:T(8,128)(2,1)} %constant.11.clone.bwd_ref), custom_call_target="tpu_custom_call" | custom-call | tf_op jit(solution)/shard_map/lat_part/pallas_call | solution.py:289
  47.7 10.7 %field_part.2 = (bf16[24,64,2048]{2,1,0:T(8,128)(2,1)}, bf16[128,24,128]{2,1,0:T(8,128)(2,1)}) custom-call(bf16[128,24,128]{2,1,0:T(8,128)(2,1)} %lat_part.2.y_ref, bf16[24,64,2048]{2,1,0:T(8,128)(2,1)} %h_ref.3, bf16[256,2048]{1,0:T(8,128)(2,1)} %constant.9.clone.back_ref, bf16[2,64,64]{2,1,0:T(8,128)(2,1)} %local_ref.3, ...), custom_call_target="tpu_custom_call" | custom-call | tf_op jit(solution)/shard_map/field_part/pallas_call | solution.py:419
  58.4 38.5 %lat_part.3.y_ref = bf16[128,24,128]{2,1,0:T(8,128)(2,1)} custom-call(bf16[128,24,128]{2,1,0:T(8,128)(2,1)} %get-tuple-element.7.x_ref, bf16[2,128,64,128]{3,2,1,0:T(8,128)(2,1)} %weight_ref.3, bf16[4,256,192]{2,1,0:T(8,128)(2,1)} %constant.10.clone.fwd_ref, bf16[4,384,128]{2,1,0:T(8,128)(2,1)} %constant.11.clone.bwd_ref), custom_call_target="tpu_custom_call" | custom-call | tf_op jit(solution)/shard_map/lat_part/pallas_call | solution.py:289
  96.8 9.5 %field_part.3 = bf16[24,64,2048]{2,1,0:T(8,128)(2,1)} custom-call(bf16[128,24,128]{2,1,0:T(8,128)(2,1)} %lat_part.3.y_ref, bf16[24,64,2048]{2,1,0:T(8,128)(2,1)} %get-tuple-element.8.h_ref, bf16[256,2048]{1,0:T(8,128)(2,1)} %constant.9.clone.back_ref, bf16[2,64,64]{2,1,0:T(8,128)(2,1)} %local_ref.3), custom_call_target="tpu_custom_call" | custom-call | tf_op jit(solution)/shard_map/field_part/pallas_call | solution.py:419

commit v4 on v3

--- a/solution.py
+++ b/solution.py
@@ -11,7 +11,7 @@
 
 KY = 128
 MESH = pl.DeviceIdType.MESH
-LAG = (0, 1, 2, 3, 4)
+LAG = (0, 1, 3, 4, 6)
 ROW_BLOCK = 8
 CHUNK = 512
 
@@ -371,9 +371,10 @@
                 pointwise[...], h_ref[first:first + span, :, cells].reshape(many, chunk),
                 preferred_element_type=jnp.float32,
             )
+            total = total.astype(jnp.bfloat16)
             curve = jnp.tanh(total * (inner + (inner * 0.044715) * (total * total)))
             out_ref[first:first + span, :, cells] = (
-                (total * (0.5 + 0.5 * curve)).astype(jnp.bfloat16).reshape(span, channels, chunk)
+                (total * (0.5 + 0.5 * curve)).reshape(span, channels, chunk)
             )
     if with_modes:
         flat = jnp.dot(

time: 107 us -> 103 us (0.963)
  Pallas kernels: 106 us -> 103 us
    pallas_call x2, Pallas kernels: 20.2 us -> 18.2 us  [field_part(): pl.pallas_call(functools.partial(field_kernel, layer, with_modes), grid=(...]
    pallas_call x2, Pallas kernels: 80.2 us -> 78.5 us  [lat_part(): pl.pallas_call(functools.partial(lat_kernel, layer, group, outer, steps,...]
where the time goes in v4:
time: 103 us
  Pallas kernels  103 us (100%)
    pallas_call x2, Pallas kernels, lat_part(): pl.pallas_call(functools.partial(lat_kernel, layer, group, outer, steps,...  78.5 us
    pallas_call x2, Pallas kernels, field_part(): pl.pallas_call(functools.partial(field_kernel, layer, with_modes), grid=(...  18.2 us
    pallas_call x1, Pallas kernels, lon_part(): pl.pallas_call(lon_kernel, grid=(rows // ROW_BLOCK,), out_shape=jax.Shape...  5.9 us

profile of v4, /device:TPU:0, one launch (start us, length us, event | category | flops | bytes accessed | tf_op | source)
XLA Modules:
  0.0 102.6 jit_solution(565322825842786029)
XLA Ops:
  0.0 5.9 %lon_part.1.x_ref = bf16[128,24,128]{2,1,0:T(8,128)(2,1)} custom-call(bf16[24,64,2048]{2,1,0:T(8,128)(2,1)} %h_ref.3, bf16[2048,256]{1,0:T(8,128)(2,1)} %constant.8.clone.table_ref.rest_0_), custom_call_target="tpu_custom_call" | custom-call | tf_op jit(solution)/shard_map/lon_part/pallas_call | solution.py:395
  5.9 41.0 %lat_part.2.y_ref = bf16[128,24,128]{2,1,0:T(8,128)(2,1)} custom-call(bf16[128,24,128]{2,1,0:T(8,128)(2,1)} %lon_part.1.x_ref, bf16[2,128,64,128]{3,2,1,0:T(8,128)(2,1)} %weight_ref.3, bf16[4,256,192]{2,1,0:T(8,128)(2,1)} %constant.10.clone.fwd_ref, bf16[4,384,128]{2,1,0:T(8,128)(2,1)} %constant.11.clone.bwd_ref), custom_call_target="tpu_custom_call" | custom-call | tf_op jit(solution)/shard_map/lat_part/pallas_call | solution.py:289
  47.0 9.5 %field_part.2 = (bf16[24,64,2048]{2,1,0:T(8,128)(2,1)}, bf16[128,24,128]{2,1,0:T(8,128)(2,1)}) custom-call(bf16[128,24,128]{2,1,0:T(8,128)(2,1)} %lat_part.2.y_ref, bf16[24,64,2048]{2,1,0:T(8,128)(2,1)} %h_ref.3, bf16[256,2048]{1,0:T(8,128)(2,1)} %constant.9.clone.back_ref, bf16[2,64,64]{2,1,0:T(8,128)(2,1)} %local_ref.3, ...), custom_call_target="tpu_custom_call" | custom-call | tf_op jit(solution)/shard_map/field_part/pallas_call | solution.py:420
  56.4 37.5 %lat_part.3.y_ref = bf16[128,24,128]{2,1,0:T(8,128)(2,1)} custom-call(bf16[128,24,128]{2,1,0:T(8,128)(2,1)} %get-tuple-element.7.x_ref, bf16[2,128,64,128]{3,2,1,0:T(8,128)(2,1)} %weight_ref.3, bf16[4,256,192]{2,1,0:T(8,128)(2,1)} %constant.10.clone.fwd_ref, bf16[4,384,128]{2,1,0:T(8,128)(2,1)} %constant.11.clone.bwd_ref), custom_call_target="tpu_custom_call" | custom-call | tf_op jit(solution)/shard_map/lat_part/pallas_call | solution.py:289
  93.9 8.8 %field_part.3 = bf16[24,64,2048]{2,1,0:T(8,128)(2,1)} custom-call(bf16[128,24,128]{2,1,0:T(8,128)(2,1)} %lat_part.3.y_ref, bf16[24,64,2048]{2,1,0:T(8,128)(2,1)} %get-tuple-element.8.h_ref, bf16[256,2048]{1,0:T(8,128)(2,1)} %constant.9.clone.back_ref, bf16[2,64,64]{2,1,0:T(8,128)(2,1)} %local_ref.3), custom_call_target="tpu_custom_call" | custom-call | tf_op jit(solution)/shard_map/field_part/pallas_call | solution.py:420

commit v5 on v4

--- a/solution.py
+++ b/solution.py
@@ -11,7 +11,7 @@
 
 KY = 128
 MESH = pl.DeviceIdType.MESH
-LAG = (0, 1, 3, 4, 6)
+LAG = (0, 1, 4, 5, 8)
 ROW_BLOCK = 8
 CHUNK = 512
 

time: 103 us -> 102 us (level)
  no operation moved by 1% of the time
where the time goes in v5:
time: 102 us
  Pallas kernels  102 us (100%)
    pallas_call x2, Pallas kernels, lat_part(): pl.pallas_call(functools.partial(lat_kernel, layer, group, outer, steps,...  77.6 us
    pallas_call x2, Pallas kernels, field_part(): pl.pallas_call(functools.partial(field_kernel, layer, with_modes), grid=(...  18.2 us
    pallas_call x1, Pallas kernels, lon_part(): pl.pallas_call(lon_kernel, grid=(rows // ROW_BLOCK,), out_shape=jax.Shape...  5.9 us

profile of v5, /device:TPU:0, one launch (start us, length us, event | category | flops | bytes accessed | tf_op | source)
XLA Modules:
  0.0 101.7 jit_solution(13085673578411569450)
XLA Ops:
  0.0 5.9 %lon_part.1.x_ref = bf16[128,24,128]{2,1,0:T(8,128)(2,1)} custom-call(bf16[24,64,2048]{2,1,0:T(8,128)(2,1)} %h_ref.3, bf16[2048,256]{1,0:T(8,128)(2,1)} %constant.8.clone.table_ref.rest_0_), custom_call_target="tpu_custom_call" | custom-call | tf_op jit(solution)/shard_map/lon_part/pallas_call | solution.py:395
  5.9 40.6 %lat_part.2.y_ref = bf16[128,24,128]{2,1,0:T(8,128)(2,1)} custom-call(bf16[128,24,128]{2,1,0:T(8,128)(2,1)} %lon_part.1.x_ref, bf16[2,128,64,128]{3,2,1,0:T(8,128)(2,1)} %weight_ref.3, bf16[4,256,192]{2,1,0:T(8,128)(2,1)} %constant.10.clone.fwd_ref, bf16[4,384,128]{2,1,0:T(8,128)(2,1)} %constant.11.clone.bwd_ref), custom_call_target="tpu_custom_call" | custom-call | tf_op jit(solution)/shard_map/lat_part/pallas_call | solution.py:289
  46.5 9.5 %field_part.2 = (bf16[24,64,2048]{2,1,0:T(8,128)(2,1)}, bf16[128,24,128]{2,1,0:T(8,128)(2,1)}) custom-call(bf16[128,24,128]{2,1,0:T(8,128)(2,1)} %lat_part.2.y_ref, bf16[24,64,2048]{2,1,0:T(8,128)(2,1)} %h_ref.3, bf16[256,2048]{1,0:T(8,128)(2,1)} %constant.9.clone.back_ref, bf16[2,64,64]{2,1,0:T(8,128)(2,1)} %local_ref.3, ...), custom_call_target="tpu_custom_call" | custom-call | tf_op jit(solution)/shard_map/field_part/pallas_call | solution.py:420
  56.0 36.9 %lat_part.3.y_ref = bf16[128,24,128]{2,1,0:T(8,128)(2,1)} custom-call(bf16[128,24,128]{2,1,0:T(8,128)(2,1)} %get-tuple-element.7.x_ref, bf16[2,128,64,128]{3,2,1,0:T(8,128)(2,1)} %weight_ref.3, bf16[4,256,192]{2,1,0:T(8,128)(2,1)} %constant.10.clone.fwd_ref, bf16[4,384,128]{2,1,0:T(8,128)(2,1)} %constant.11.clone.bwd_ref), custom_call_target="tpu_custom_call" | custom-call | tf_op jit(solution)/shard_map/lat_part/pallas_call | solution.py:289
  92.9 8.8 %field_part.3 = bf16[24,64,2048]{2,1,0:T(8,128)(2,1)} custom-call(bf16[128,24,128]{2,1,0:T(8,128)(2,1)} %lat_part.3.y_ref, bf16[24,64,2048]{2,1,0:T(8,128)(2,1)} %get-tuple-element.8.h_ref, bf16[256,2048]{1,0:T(8,128)(2,1)} %constant.9.clone.back_ref, bf16[2,64,64]{2,1,0:T(8,128)(2,1)} %local_ref.3), custom_call_target="tpu_custom_call" | custom-call | tf_op jit(solution)/shard_map/field_part/pallas_call | solution.py:420
